TPU v7x, 512 devices: a whole 4x8x8 slice. The times are simulated.
512 devices in a mesh: ka: 64 (over x, y, core), ta: 8 (over z).
Axes of the slice: x: 4, y: 8, z: 8, core: 2. Of those that a mesh axis runs over, the one named last changes fastest.
Arguments:
- sigma_history: bfloat16 [128, 4096, 256], P('ka', 'ta'), may hold values from -6 to 6
- time_basis: bfloat16 [4096, 64], P('ta'), may hold values from -0.75 to 0.75
- history_coef: bfloat16 [128, 512, 256], P('ka', 'ta'), may hold values from -6 to 6
- green_now: float32 [128, 256], P('ka'), may hold values from -6 to 6
- hamilton: float32 [128, 256], P('ka'), may hold values from -1.5 to 1.5
- panel_block: bfloat16 [128, 2048, 2048], P('ka', 'ta'), may hold values from -7 to 7
- panel_lengths: int32 [8], P('ta'), may hold values from 1 to 16, 120 in all
- owners: int32 [128, 1], P('ka'), may hold values from 0 to 15
- sketch: bfloat16 [16, 2048, 64], P(None, 'ka'), may hold values from -6 to 6
Outputs:
- green_next: float32 [128, 256], P('ka')
- ortho_factor: float32 [128, 2048, 64], P('ka', 'ta')
- coef_factor: float32 [128, 64, 2048], P('ka', None, 'ta')
Inputs may be any that keep to these rules, and one draw needn't show every extreme that they name: `owners`: every compressor rank serves some k-point. `panel_lengths`: they sum to 120; the largest is 16.
All inputs are finite; a program needn't handle non-finite values. No bound on the sum of `panel_lengths` on one device may be relied on, other than what follows from the above.
Results may differ from a plain program's by a relative error of at most 0.0095.
Values may be sent and summed in bfloat16 or wider, within the bound.
No kernel may reach another device: no remote copies, remote signals or barrier semaphores. Data moves between devices by JAX's collectives and lax.ppermute only.
A program may use at most 64 MiB of HBM per device.

v0:
```python
import math

import jax
import jax.numpy as jnp
from jax import lax
from jax.sharding import PartitionSpec as P

NO = 16
R = 64
PROW_DEV = 16


step_size = 0.25


def prefix(value, axis, join, neutral):
    count, mine = (lax.axis_size(axis), lax.axis_index(axis))
    pieces = lax.all_gather(value, axis)
    running = jnp.full_like(value, 0) + jnp.asarray(neutral, value.dtype)

    def step(position, running):
        longer = join(running, pieces[position])
        return jnp.where(position < mine, longer, running)

    return lax.fori_loop(0, count - 1, step, running)


def add_counts(earlier, later):
    return earlier + later


def compress_panels(sketched, tri_panel):
    gram = jnp.einsum("srq,srp->sqp", sketched, sketched, precision=lax.Precision.HIGHEST)
    gram_total = lax.psum(gram, "ta")
    lower_factor = jnp.linalg.cholesky(gram_total)
    ortho = lax.linalg.triangular_solve(
        lower_factor, sketched, left_side=False, lower=True, transpose_a=True
    )
    coeffs = jnp.einsum(
        "srq,src->sqc", ortho.astype(jnp.bfloat16), tri_panel, preferred_element_type=jnp.float32
    )
    coef_total = lax.psum_scatter(
        coeffs.astype(jnp.bfloat16), "ta", scatter_dimension=2, tiled=True
    ).astype(jnp.float32)
    return (ortho, coef_total)


def body(
    sigma_history,
    time_basis,
    history_coef,
    green_now,
    hamilton,
    panel_block,
    panel_lengths,
    owners,
    sketch,
):
    high = lax.Precision.HIGHEST
    ta_count = lax.axis_size("ta")
    k_local = green_now.shape[0]
    summed = jnp.einsum(
        "jr,kjo->kro", time_basis, sigma_history, preferred_element_type=jnp.float32
    )
    summed = summed.reshape(k_local, R, NO, NO)
    coef_local = history_coef.astype(jnp.float32).reshape(k_local, R, NO, NO)
    block_part = jnp.einsum("krac,krcd->kad", summed, coef_local, precision=high).reshape(
        k_local, NO * NO
    )
    integral = lax.psum(block_part, "ta").reshape(k_local, NO, NO)
    integral = integral / math.sqrt(NO * sigma_history.shape[1] * ta_count)
    green = green_now.reshape(k_local, NO, NO)
    hmat = hamilton.reshape(k_local, NO, NO)
    for repeat in range(2):
        left_prod = jnp.einsum("kac,kcd->kad", hmat, green, precision=high)
        right_prod = jnp.einsum("kac,kcd->kad", green, hmat, precision=high)
        green = green + step_size * (left_prod - right_prod + integral)
    green_next = green.reshape(k_local, NO * NO)
    starts = prefix(panel_lengths, "ta", add_counts, jnp.zeros((1,), jnp.int32))
    begin = starts[0]
    length = panel_lengths[0]
    slot_index = jnp.arange(PROW_DEV, dtype=jnp.int32)
    row_time = begin + slot_index
    live_rows = slot_index < length
    col_count = panel_block.shape[2]
    col_time = jnp.arange(col_count, dtype=jnp.int32) // NO - PROW_DEV // 2
    keep = live_rows[:, None, None] & (col_time[None, None, :] <= row_time[:, None, None])
    keep = jnp.broadcast_to(keep, (PROW_DEV, NO, col_count)).reshape(PROW_DEV * NO, col_count)
    tri_panel = jnp.where(keep[None], panel_block, jnp.zeros_like(panel_block))
    owner_ids = owners[:, 0]
    rank_count = sketch.shape[0]
    pick = (owner_ids[:, None] == jnp.arange(rank_count, dtype=jnp.int32)[None, :]).astype(
        jnp.bfloat16
    )
    chosen = jnp.einsum(
        "ks,scq->kcq",
        pick,
        lax.all_gather(sketch, "ka", axis=1, tiled=True),
        preferred_element_type=jnp.float32,
    ).astype(jnp.bfloat16)
    sketched = jnp.einsum("krc,kcq->krq", tri_panel, chosen, preferred_element_type=jnp.float32)
    ortho_factor, coef_factor = compress_panels(sketched, tri_panel)
    return (green_next, ortho_factor, coef_factor)


def solution(mesh):
    in_specs = (
        P("ka", "ta", None),
        P("ta", None),
        P("ka", "ta", None),
        P("ka", None),
        P("ka", None),
        P("ka", "ta", None),
        P("ta"),
        P("ka", None),
        P(None, "ka", None),
    )
    out_specs = (P("ka", None), P("ka", "ta", None), P("ka", None, "ta"))
    return jax.shard_map(body, mesh=mesh, in_specs=in_specs, out_specs=out_specs, check_vma=False)
```

profile of v0, /device:TPU:6, one launch (start us, length us, event | category | flops | bytes accessed | tf_op | source)
XLA Modules:
  0.0 220.3 jit_solution(14134690025183436860)
XLA Ops:
  7.2 0.0 copy-start
  7.2 0.0 all-gather.3.cloned.1.call-start
  7.2 1.7 copy.42
  8.9 0.0 all-gather.3.cloned.1.call-update
  8.9 0.0 reduce-scatter.2.cloned.1.call-start
  9.6 1.3 dynamic-slice
  10.9 0.8 dynamic-update-slice.3
  11.6 18.8 %all-reduce = s32[8]{0:T(128)S(1)} all-reduce(s32[8]{0:T(128)S(1)} %dynamic-update-slice.3), channel_id=2, replica_groups=mesh['ka'=64,'ta'=8] {'ta'}, use_global_device_ids=true, to_apply=%add | all-reduce | flops 8 | bytes 64
  30.5 0.8 reshape.110
  31.2 0.8 reshape.109
  32.0 1.0 convolution_bitcast_fusion
  33.1 0.1 copy.37
  33.2 1.0 copy.38
  34.2 0.4 convolution_bitcast_fusion.2
  34.5 0.1 reshape.113
  34.6 8.7 %while.13 = (s32[]{:T(128)}, s32[1]{0:T(128)}, s32[]{:T(128)}, s32[8,1]{0,1:T(1,128)S(1)}, s32[]{:T(128)}) while((s32[]{:T(128)}, s32[1]{0:T(128)}, s32[]{:T(128)}, s32[8,1]{0,1:T(1,128)S(1)}, s32[]{:T(128)}) %tuple.39), condition=%wide.region_2.3_spmd, body=%wide.region_1.2_spmd.sunk | while | flops 5 | bytes 115 | solution.py:25
  34.6 0.6 constant_dynamic-slice_fusion.2
  35.9 0.6 constant_dynamic-slice_fusion.2
  37.1 0.6 constant_dynamic-slice_fusion.2
  38.4 0.6 constant_dynamic-slice_fusion.2
  39.6 0.6 constant_dynamic-slice_fusion.2
  40.9 0.6 constant_dynamic-slice_fusion.2
  42.1 0.6 constant_dynamic-slice_fusion.2
  43.4 0.1 compare_and_fusion
  43.5 0.0 copy-start.2
  43.5 59.5 %all-gather.3.cloned.1.call-done = bf16[16,2048,64]{2,0,1:T(8,128)(2,1)} async-done(((bf16[16,32,64]{2,0,1:T(8,128)(2,1)}), bf16[16,2048,64]{2,0,1:T(8,128)(2,1)}) %all-gather.3.cloned.1.call-update) | async-done | bytes 4194320 | tf_op jit(solution)/shard_map/all_gather | solution.py:98
  103.0 12.0 %copy.43 = bf16[16,2048,64]{1,0,2:T(8,128)(2,1)} copy(bf16[16,2048,64]{2,0,1:T(8,128)(2,1)} %all-gather.3.cloned.1.call-done) | data formatting | bytes 8388608 | tf_op jit(solution)/shard_map/all_gather | solution.py:98
  115.0 3.2 %convolution_convert_fusion.1 = bf16[2,2048,64]{1,0,2:T(2,128)(2,1)S(1)} fusion(bf16[16,2048,64]{1,0,2:T(8,128)(2,1)} %copy.43, s32[2]{0:T(128)S(1)} %bitcast.55), kind=kOutput, calls=%fused_computation.2 | convolution fusion | flops 8650784 | bytes 4718600 | tf_op jit(solution)/shard_map/ks,scq->kcq/dot_general | solution.py:95
  118.2 0.2 broadcast_in_dim.26
  118.5 0.8 fusion
  119.2 0.3 fusion.27
  119.5 31.7 %all-reduce.1 = (f32[2,256]{1,0:T(2,128)S(1)}, f32[2,64,64]{1,2,0:T(8,128)S(1)}) all-reduce(f32[2,256]{1,0:T(2,128)S(1)} %reshape.113, f32[2,64,64]{1,2,0:T(8,128)S(1)} %fusion.27), channel_id=1, replica_groups=mesh['ka'=64,'ta'=8] {'ta'}, use_global_device_ids=true, to_apply=%region_0.0 | all-reduce | flops 8704 | bytes 69632 | tf_op jit(solution)/shard_map/psum | solution.py:70
  151.2 0.1 copy.46
  151.3 11.7 %custom-call.7 = f32[2,64,64]{2,1,0:T(8,128)S(1)} custom-call(f32[2,64,64]{2,1,0:T(8,128)S(1)} %fusion.13), custom_call_target="Cholesky" | custom-call | tf_op jit(solution)/shard_map/jit(cholesky)/cholesky | solution.py:35
  163.1 0.1 compare_reduce_fusion
  163.2 0.1 select_bitcast_fusion
  163.3 9.8 %custom-call.8 = f32[2,1,64,64]{2,3,1,0:T(8,128)S(1)} custom-call(f32[2,1,64,64]{3,2,1,0:T(8,128)S(1)} %select_bitcast_fusion), custom_call_target="InvertDiagBlocksLowerTriangular" | custom-call | tf_op jit(solution)/shard_map/triangular_solve | solution.py:36
  173.1 0.3 fusion.11
  173.5 1.4 convolution_convert_fusion
  174.8 0.0 reduce-scatter.2.cloned.1.call-update
  174.9 0.1 fusion.26
  175.0 0.1 div.26
  175.1 0.2 fusion.6
  175.2 0.2 convolution_bitcast_fusion.1
  175.4 0.1 fusion.3
  175.5 0.7 reshape.114
  176.2 35.7 %reduce-scatter.2.cloned.1.call-done = bf16[2,64,256]{2,1,0:T(8,128)(2,1)} async-done(((bf16[2,64,2048]{2,1,0:T(8,128)(2,1)}), bf16[2,64,256]{2,1,0:T(8,128)(2,1)}) %reduce-scatter.2.cloned.1.call-update) | async-done | bytes 65552 | tf_op jit(solution)/shard_map/reduce_scatter | solution.py:42
  211.9 1.5 convert_element_type.17
  (15 shorter events, 0.1 us)
Async XLA Ops:
  7.2 24.8 %copy-start = (bf16[2,512,256]{2,1,0:T(8,128)(2,1)S(1)}, bf16[2,512,256]{2,1,0:T(8,128)(2,1)}, u32[]{:S(2)}) copy-start(bf16[2,512,256]{2,1,0:T(8,128)(2,1)} %param.11) | copy-start | bytes 1572868
  7.2 95.8 %all-gather.3.cloned.1.call-start = ((), (), s32[]{:S(2)}) async-start(), calls=%async_computation.1 | async-start | bytes 8519680 | tf_op jit(solution)/shard_map/all_gather | solution.py:98
  8.9 203.0 %reduce-scatter.2.cloned.1.call-start = ((), (), s32[]{:S(2)}) async-start(), calls=%async_computation.2 | async-start | bytes 589824 | tf_op jit(solution)/shard_map/reduce_scatter | solution.py:42
  43.5 71.5 %copy-start.2 = (s32[2,1]{0,1:T(1,128)S(1)}, s32[2,1]{0,1:T(1,128)}, u32[]{:S(2)}) copy-start(s32[2,1]{0,1:T(1,128)} %param.18) | copy-start | bytes 28
  115.0 3.4 %copy-start.3 = (bf16[2,256,2048]{2,1,0:T(8,128)(2,1)S(1)}, bf16[2,256,2048]{2,1,0:T(8,128)(2,1)}, u32[]{:S(2)}) copy-start(bf16[2,256,2048]{2,1,0:T(8,128)(2,1)} %param.16) | copy-start | bytes 6291460
  173.5 1.4 copy-start.1
Sparse Core Ops, SparseCore 0:
  11.9 91.0 all-gather.2
  175.0 36.9 reduce-scatter.1
where the time goes:
time: 221 us; the launch traced here: 220 us
  waiting for transfers between devices  95.3 us (43%)
  blocking collectives  50.5 us (23%)
  local copies, waits for them, and re-layouts  23.7 us (11%)
  other arithmetic  23.4 us (11%)
  between operations  14.9 us (7%)
  matrix products  7.87 us (4%)
  loops' own time  4.57 us (2%)
    all_gather x1, waiting for transfers between devices, body(): lax.all_gather(sketch, 'ka', axis=1, tiled=True)  59.5 us
    reduce_scatter x1, waiting for transfers between devices, compress_panels(): lax.psum_scatter(coeffs.astype(jnp.bfloat16), 'ta', scatter_dimension=2,...  35.7 us
    psum x1, blocking collectives, body(): integral = lax.psum(block_part, 'ta').reshape(k_local, NO, NO)  31.7 us
    unnamed x1, blocking collectives  18.8 us
    all_gather x1, local copies, waits for them, and re-layouts, body(): lax.all_gather(sketch, 'ka', axis=1, tiled=True)  12 us
    another operation x4, other arithmetic, compress_panels(): lower_factor = jnp.linalg.cholesky(gram_total)  11.9 us
    another operation x3, other arithmetic, compress_panels(): lax.linalg.triangular_solve(lower_factor, sketched, left_side=False, lowe...  9.92 us
    unnamed x13, local copies, waits for them, and re-layouts  4.68 us
  transfers between devices with their start and end apart: 2, of which 2 were waited for; matrix products, arithmetic and copies ran while one was open for 5% of the time, Pallas kernels for 0%

commit v1 on v0

v1 whole, which is shorter than its diff:
```python
import jax
import jax.numpy as jnp
from jax import lax
from jax.experimental import pallas as pl
from jax.experimental.pallas import tpu as pltpu
from jax.sharding import PartitionSpec as P

NO = 16
OO = NO * NO
R = 64
SLOTS = 16
LANES = 128
STEP = 0.25
HIGH = lax.Precision.HIGHEST
F32 = jnp.float32
BF16 = jnp.bfloat16


def dot(left, right, contract, precision=None):
    return lax.dot_general(
        left, right, (contract, ((), ())), precision=precision, preferred_element_type=F32
    )


def iota(shape, dim):
    return lax.broadcasted_iota(jnp.int32, shape, dim)


def pick_rows(ka_count, ta_count, told, sketch):
    def kernel(told, me, sketch, picked, facts, double):
        for rank in range(sketch.shape[0]):
            rows = sketch[rank]
            double[rank] = jnp.concatenate([rows, rows], axis=1)
        left = iota(double.shape[1:], 1) < R

        def one(place, carry):
            picked[place] = jnp.where(left, double[told[place, 0]], double[told[place, 1]])
            return carry

        lax.fori_loop(0, ka_count, one, 0, unroll=8)
        begin = jnp.int32(0)
        length = jnp.int32(0)
        for place in range(ta_count):
            where_from, amount = told[place, 3], told[place, 2]
            begin = begin + jnp.where(where_from < me[0], amount, 0)
            length = length + jnp.where(where_from == me[0], amount, 0)
        facts[0] = begin
        facts[1] = length

    ranks, rows, _ = sketch.shape
    smem = pl.BlockSpec(memory_space=pltpu.SMEM)
    vmem = pl.BlockSpec(memory_space=pltpu.VMEM)
    me = lax.axis_index("ta").astype(jnp.int32).reshape(1)
    return pl.pallas_call(
        kernel,
        out_shape=(
            jax.ShapeDtypeStruct((ka_count, rows, LANES), BF16),
            jax.ShapeDtypeStruct((2,), jnp.int32),
        ),
        in_specs=[smem, smem, vmem],
        out_specs=(vmem, smem),
        scratch_shapes=[pltpu.VMEM((ranks, rows, LANES), BF16)],
        compiler_params=pltpu.CompilerParams(vmem_limit_bytes=8 << 20),
        name="pick_rows",
    )(told, me, sketch)


def keep_mask(facts, rows, cols):
    slot = iota((rows, 1), 0) >> 4
    top = jnp.where(slot < facts[1], facts[0] + slot + SLOTS // 2, -1)
    group = iota((1, cols), 1) >> 4
    return group.astype(F32).astype(BF16) <= top.astype(F32).astype(BF16)


def sketch_panels(facts, chosen, panel, sigma, basis, coef, copies):
    def kernel(facts, chosen, panel, sigma, basis, coef, sketched, shared):
        k_count, rows, cols = panel.shape
        keep = keep_mask(facts, rows, cols)
        zero = jnp.zeros((rows, cols), BF16)
        parts = [
            dot(jnp.where(keep, panel[k], zero), chosen[...], ((1,), (0,))) for k in range(k_count)
        ]
        both = jnp.where(iota((rows, LANES), 1) < R, parts[0], parts[1])
        sketched[...] = both
        square = dot(both, both, ((0,), (0,)), HIGH)
        gram = jnp.where(iota((R, LANES), 1) < R, square[:R], square[R:])

        row, col = iota((OO, OO), 0), iota((OO, OO), 1)
        inner = (row & 15) == (col >> 4)
        spread = jnp.where((row & 15) == (col & 15), 1.0, 0.0).astype(F32)
        same = (row >> 4) == (col >> 4)
        lines = []
        for k in range(k_count):
            summed = dot(basis[...], sigma[k], ((1,), (0,)))
            pairs = dot(summed, coef[k].astype(F32), ((0,), (0,)), HIGH)
            laid = dot(jnp.where(inner, pairs, 0.0), spread, ((1,), (0,)), HIGH)
            line = jnp.sum(jnp.where(same, laid, 0.0), axis=0, keepdims=True)
            lines += [line[:, :LANES], line[:, LANES:]]
        tail = jnp.concatenate(lines + [jnp.zeros((4, LANES), F32)], axis=0)
        for place in range(copies):
            shared[place, :R] = gram
            shared[place, R:] = tail

    k_count, rows, cols = panel.shape
    smem = pl.BlockSpec(memory_space=pltpu.SMEM)
    vmem = pl.BlockSpec(memory_space=pltpu.VMEM)
    return pl.pallas_call(
        kernel,
        out_shape=(
            jax.ShapeDtypeStruct((rows, LANES), F32),
            jax.ShapeDtypeStruct((copies, R + 8, LANES), F32),
        ),
        in_specs=[smem] + [vmem] * 5,
        out_specs=(vmem, vmem),
        compiler_params=pltpu.CompilerParams(vmem_limit_bytes=20 << 20),
        name="sketch_panels",
    )(facts, chosen, panel, sigma, basis, coef)


def inverse_factor(work, offset):
    lane = iota((R, LANES), 1)
    row = iota((R, 1), 0)
    diag = jnp.zeros((R, 1), F32)
    for step in range(R):
        low = (step // 8) * 8
        part = work[low:]
        line = work[step : step + 1]
        pivot = line[:, offset + step : offset + step + 1]
        scale = part[:, offset + step : offset + step + 1] * (1.0 / pivot)
        scale = jnp.where(row[low:] > step, scale, 0.0)
        diag = jnp.where(row == step, pivot, diag)
        part = part - scale * line
        work = part if low == 0 else jnp.concatenate([work[:low], part], axis=0)
    return work * lax.rsqrt(diag), lane


def finish_panels(facts, told, sketched, panel, green, hamilton, chunk):
    def kernel(facts, told, sketched, panel, green, hamilton, next_green, ortho, terms):
        k_count, rows, cols = panel.shape
        total = told[0]
        for place in range(1, told.shape[0]):
            total = total + told[place]
        gram = total[:R]
        lane = iota((R, LANES), 1)
        left = lane < R
        eye = jnp.where((lane & (R - 1)) == iota((R, LANES), 0), 1.0, 0.0).astype(F32)
        first, _ = inverse_factor(jnp.where(left, gram, eye), 0)
        second, _ = inverse_factor(jnp.where(left, eye, gram), R)
        zero = jnp.zeros((R, LANES), F32)
        factor = jnp.concatenate(
            [
                jnp.where(left, pltpu.roll(first, R, 1), zero),
                jnp.where(left, zero, pltpu.roll(second, R, 1)),
            ],
            axis=0,
        )
        both = dot(factor, sketched[...], ((1,), (1,)), HIGH)
        ortho[0] = both[:R]
        ortho[1] = both[R:]
        rounded = both.astype(BF16)
        keep = keep_mask(facts, rows, cols)
        blank = jnp.zeros((rows, cols), BF16)
        for k in range(k_count):
            coeffs = dot(rounded, jnp.where(keep, panel[k], blank), ((1,), (0,)))
            coeffs = coeffs[k * R : (k + 1) * R].astype(BF16)
            for place in range(cols // chunk):
                for half in range(chunk // LANES):
                    at = place * chunk + half * LANES
                    base = (k * (chunk // LANES) + half) * R
                    terms[place, base : base + R] = coeffs[:, at : at + LANES]

        outer = (iota((NO, OO), 1) >> 4) == iota((NO, OO), 0)
        tile = jnp.where((iota((NO, OO), 1) & 15) == iota((NO, OO), 0), 1.0, 0.0).astype(F32)

        def square(line):
            return dot(jnp.where(outer, line, 0.0), tile, ((1,), (1,)), HIGH)

        for k in range(k_count):
            base = R + 2 * k
            line = jnp.concatenate([total[base : base + 1], total[base + 1 : base + 2]], axis=1)
            rate = square(line) * (1.0 / 256.0)
            g, h = square(green[k : k + 1]), square(hamilton[k : k + 1])
            for _ in range(2):
                left_prod = dot(h, g, ((1,), (0,)), HIGH)
                right_prod = dot(g, h, ((1,), (0,)), HIGH)
                g = g + STEP * (left_prod - right_prod + rate)
            flat = jnp.where(outer, dot(g, tile, ((1,), (0,)), HIGH), 0.0)
            next_green[k : k + 1] = jnp.sum(flat, axis=0, keepdims=True)

    k_count, rows, cols = panel.shape
    smem = pl.BlockSpec(memory_space=pltpu.SMEM)
    vmem = pl.BlockSpec(memory_space=pltpu.VMEM)
    return pl.pallas_call(
        kernel,
        out_shape=(
            jax.ShapeDtypeStruct((k_count, OO), F32),
            jax.ShapeDtypeStruct((k_count, R, rows), F32),
            jax.ShapeDtypeStruct((cols // chunk, k_count * R * chunk // LANES, LANES), BF16),
        ),
        in_specs=[smem] + [vmem] * 5,
        out_specs=(vmem, vmem, vmem),
        compiler_params=pltpu.CompilerParams(vmem_limit_bytes=20 << 20),
        name="finish_panels",
    )(facts, told, sketched, panel, green, hamilton)


def add_terms(told, k_count, chunk):
    def kernel(told, out):
        total = told[0].astype(F32)
        for place in range(1, told.shape[0]):
            total = total + told[place].astype(F32)
        halves = chunk // LANES
        for k in range(k_count):
            for half in range(halves):
                base = (k * halves + half) * R
                out[k, :, half * LANES : (half + 1) * LANES] = total[base : base + R]

    vmem = pl.BlockSpec(memory_space=pltpu.VMEM)
    return pl.pallas_call(
        kernel,
        out_shape=jax.ShapeDtypeStruct((k_count, R, chunk), F32),
        in_specs=[vmem],
        out_specs=vmem,
        compiler_params=pltpu.CompilerParams(vmem_limit_bytes=8 << 20),
        name="add_terms",
    )(told)


def body(
    sigma_history,
    time_basis,
    history_coef,
    green_now,
    hamilton,
    panel_block,
    panel_lengths,
    owners,
    sketch,
):
    ka_count, ta_count = lax.axis_size("ka"), lax.axis_size("ta")
    k_count = green_now.shape[0]
    assert NO * sigma_history.shape[1] * ta_count == 65536 and k_count == 2
    groups = [
        [place * ta_count + (group + place) % ta_count for place in range(ka_count)]
        for group in range(ta_count)
    ]
    facts = jnp.concatenate(
        [owners[:, 0], panel_lengths, lax.axis_index("ta").astype(jnp.int32).reshape(1)]
    )
    facts = jnp.pad(facts, (0, LANES - 4))
    told = lax.all_to_all(
        jnp.broadcast_to(facts[None, None], (ka_count, 1, LANES)),
        ("ka", "ta"),
        0,
        0,
        axis_index_groups=groups,
    ).reshape(ka_count, LANES)
    picked, facts = pick_rows(ka_count, ta_count, told, sketch)
    chosen = lax.all_to_all(picked, "ka", 0, 0).reshape(-1, LANES)
    sketched, shared = sketch_panels(
        facts, chosen, panel_block, sigma_history, time_basis.T, history_coef, ta_count
    )
    told = lax.all_to_all(shared, "ta", 0, 0)
    chunk = panel_block.shape[2] // ta_count
    green_next, ortho, terms = finish_panels(
        facts, told, sketched, panel_block, green_now, hamilton, chunk
    )
    told = lax.all_to_all(terms, "ta", 0, 0)
    return (green_next, ortho.transpose(0, 2, 1), add_terms(told, k_count, chunk))


def solution(mesh):
    in_specs = (
        P("ka", "ta", None),
        P("ta", None),
        P("ka", "ta", None),
        P("ka", None),
        P("ka", None),
        P("ka", "ta", None),
        P("ta"),
        P("ka", None),
        P(None, "ka", None),
    )
    out_specs = (P("ka", None), P("ka", "ta", None), P("ka", None, "ta"))
    return jax.shard_map(body, mesh=mesh, in_specs=in_specs, out_specs=out_specs, check_vma=False)
```

time: 221 us -> 113 us (0.51)
  waiting for transfers between devices: 95.3 us -> 0 us
  blocking collectives: 50.5 us -> 90.1 us
  other arithmetic: 23.4 us -> 0.73 us
  local copies, waits for them, and re-layouts: 23.7 us -> 5.28 us
  Pallas kernels: 0 us -> 14.7 us
  between operations: 14.9 us -> 1.31 us
  matrix products: 7.87 us -> 0 us
  loops' own time: 4.57 us -> 0 us
    all_to_all x0 -> x4, blocking collectives: none -> 90.1 us  [the longest x1 28 us: body(): lax.all_to_all(jnp.broadcast_to(facts[None, None], (ka_count, 1, LANES)),...]
    all_gather x1 -> x0, waiting for transfers between devices: 59.5 us -> none  [body(): lax.all_gather(sketch, 'ka', axis=1, tiled=True)]
    reduce_scatter x1 -> x0, waiting for transfers between devices: 35.7 us -> none  [compress_panels(): lax.psum_scatter(coeffs.astype(jnp.bfloat16), 'ta', scatter_dimension=2,...]
    psum x1 -> x0, blocking collectives: 31.7 us -> none  [body(): integral = lax.psum(block_part, 'ta').reshape(k_local, NO, NO)]
    another operation x7 -> x0, other arithmetic: 21.8 us -> none  [the longest x4 11.9 us: compress_panels(): lower_factor = jnp.linalg.cholesky(gram_total)]
    unnamed x1 -> x0, blocking collectives: 18.8 us -> none
    pallas_call x0 -> x4, Pallas kernels: none -> 14.7 us  [the longest x1 8.68 us: finish_panels(): pl.pallas_call(kernel, out_shape=(jax.ShapeDtypeStruct((k_count, OO), F32...]
    all_gather x1 -> x0, local copies, waits for them, and re-layouts: 12 us -> none  [body(): lax.all_gather(sketch, 'ka', axis=1, tiled=True)]
  transfers between devices with their start and end apart: 2 -> 0, of which waited for: 2 -> 0; matrix products, arithmetic and copies ran while one was open for 5% -> 0% of each run, Pallas kernels for 0% -> 0%
where the time goes in v1:
time: 113 us; the launch traced here: 112 us
  blocking collectives  90.1 us (80%)
  Pallas kernels  14.7 us (13%)
  local copies, waits for them, and re-layouts  5.28 us (5%)
  between operations  1.31 us (1%)
    all_to_all x1, blocking collectives, body(): lax.all_to_all(jnp.broadcast_to(facts[None, None], (ka_count, 1, LANES)),...  28 us
    all_to_all x1, blocking collectives, body(): chosen = lax.all_to_all(picked, 'ka', 0, 0).reshape(-1, LANES)  24.1 us
    all_to_all x1, blocking collectives, body(): told = lax.all_to_all(terms, 'ta', 0, 0)  20 us
    all_to_all x1, blocking collectives, body(): told = lax.all_to_all(shared, 'ta', 0, 0)  17.9 us
    pallas_call x1, Pallas kernels, finish_panels(): pl.pallas_call(kernel, out_shape=(jax.ShapeDtypeStruct((k_count, OO), F32...  8.68 us
    unnamed x16, local copies, waits for them, and re-layouts  5.25 us
    pallas_call x1, Pallas kernels, sketch_panels(): pl.pallas_call(kernel, out_shape=(jax.ShapeDtypeStruct((rows, LANES), F32...  3.25 us

profile of v1, /device:TPU:6, one launch (start us, length us, event | category | flops | bytes accessed | tf_op | source)
XLA Modules:
  0.0 112.1 jit_solution(4297378561843558918)
XLA Ops:
  1.3 0.7 pad_add_fusion
  2.0 28.0 %all_to_all.20 = s32[64,1,128]{2,1,0:T(1,128)S(1)} all-to-all(s32[64,1,128]{2,1,0:T(1,128)S(1)} %broadcast_in_dim.2), channel_id=1, replica_groups={{0,9,18,27,36,45,54,63,64,73,82,91,100,109,118,127,128,137,146,155,164,..., dimensions={0} | all-to-all | bytes 65536 | tf_op jit(solution)/shard_map/all_to_all | solution.py:251
  30.1 0.0 copy-start.3
  30.1 0.9 copy-done.3
  31.0 2.0 %pick_rows.1 = (bf16[64,32,128]{2,1,0:T(8,128)(2,1)S(1)}, s32[2]{0:T(128)S(1)}) custom-call(s32[64,128]{1,0:T(8,128)S(1)} %bitcast.7, s32[1]{0:T(128)} %bitcast.1.me, bf16[16,32,64]{2,1,0:T(8,128)(2,1)S(1)} %copy-done.3), custom_call_target="tpu_custom_call" | custom-call | tf_op jit(solution)/shard_map/pick_rows/pallas_call | solution.py:54
  33.0 24.1 %all_to_all.21 = bf16[64,32,128]{2,1,0:T(8,128)(2,1)S(1)} all-to-all(bf16[64,32,128]{2,1,0:T(8,128)(2,1)S(1)} %get-tuple-element.11), channel_id=1, replica_groups=mesh['ka'=64,'ta'=8] {'ka'}, dimensions={0} | all-to-all | bytes 1048576 | tf_op jit(solution)/shard_map/all_to_all | solution.py:259
  57.1 0.0 copy-start.6
  57.1 0.0 copy-start.7
  57.1 0.0 copy-start
  57.1 1.6 %copy-done = bf16[2,256,2048]{2,1,0:T(8,128)(2,1)S(1)} copy-done((bf16[2,256,2048]{2,1,0:T(8,128)(2,1)S(1)}, bf16[2,256,2048]{2,1,0:T(8,128)(2,1)}, u32[]{:S(2)}) %copy-start) | copy-done | bytes 2097176
  58.7 0.0 copy-start.2
  58.7 1.0 copy-done.2
  59.8 0.0 copy-start.4
  59.8 0.8 copy-done.4
  60.6 0.0 copy-start.5
  60.6 0.8 copy-done.5
  61.5 0.0 copy-start.1
  61.5 3.2 %sketch_panels.1 = (f32[256,128]{1,0:T(8,128)S(1)}, f32[8,72,128]{2,1,0:T(8,128)S(1)}) custom-call(s32[2]{0:T(128)S(1)} %get-tuple-element.10.facts, bf16[2048,128]{1,0:T(8,128)(2,1)S(1)} %bitcast.6, bf16[2,256,2048]{2,1,0:T(8,128)(2,1)S(1)} %copy-done, bf16[2,512,256]{2,1,0:T(8,128)(2,1)S(1)} %copy-done.2, bf16[64,512]{1,0:T(8,128)(2,1)S(1)} %bitcast.8, ...), custom_call_target="tpu_custom_call" | custom-call | tf_op jit(solution)/shard_map/sketch_panels/pallas_call | solution.py:107
  64.7 17.9 %all_to_all.22.told = f32[8,72,128]{2,1,0:T(8,128)S(1)} all-to-all(f32[8,72,128]{2,1,0:T(8,128)S(1)} %get-tuple-element.12), channel_id=1, replica_groups=mesh['ka'=64,'ta'=8] {'ta'}, dimensions={0} | all-to-all | bytes 589824 | tf_op jit(solution)/shard_map/all_to_all | solution.py:263
  82.7 0.0 copy-done.6
  82.7 0.0 copy-done.7
  82.7 0.0 copy-done.1
  82.7 8.7 %finish_panels.1 = (f32[2,256]{1,0:T(2,128)}, f32[2,64,256]{2,1,0:T(8,128)}, bf16[8,256,128]{2,1,0:T(8,128)(2,1)S(1)}) custom-call(s32[2]{0:T(128)S(1)} %get-tuple-element.10.facts, f32[8,72,128]{2,1,0:T(8,128)S(1)} %all_to_all.22.told, f32[256,128]{1,0:T(8,128)S(1)} %get-tuple-element.13.sketched, bf16[2,256,2048]{2,1,0:T(8,128)(2,1)S(1)} %copy-done.1, ...), custom_call_target="tpu_custom_call" | custom-call | tf_op jit(solution)/shard_map/finish_panels/pallas_call | solution.py:193
  91.3 20.0 %all_to_all.23.told = bf16[8,256,128]{2,1,0:T(8,128)(2,1)S(1)} all-to-all(bf16[8,256,128]{2,1,0:T(8,128)(2,1)S(1)} %get-tuple-element.16), channel_id=1, replica_groups=mesh['ka'=64,'ta'=8] {'ta'}, dimensions={0} | all-to-all | bytes 1048576 | tf_op jit(solution)/shard_map/all_to_all | solution.py:268
  111.3 0.7 add_terms.1
  (2 shorter events, 0.0 us)
Async XLA Ops:
  30.1 0.9 copy-start.3
  57.1 25.5 %copy-start.6 = (f32[2,256]{1,0:T(2,128)S(1)}, f32[2,256]{1,0:T(2,128)}, u32[]{:S(2)}) copy-start(f32[2,256]{1,0:T(2,128)} %green.1) | copy-start | bytes 6148
  57.1 25.5 %copy-start.7 = (f32[2,256]{1,0:T(2,128)S(1)}, f32[2,256]{1,0:T(2,128)}, u32[]{:S(2)}) copy-start(f32[2,256]{1,0:T(2,128)} %hamilton.1) | copy-start | bytes 6148
  57.1 1.6 %copy-start = (bf16[2,256,2048]{2,1,0:T(8,128)(2,1)S(1)}, bf16[2,256,2048]{2,1,0:T(8,128)(2,1)}, u32[]{:S(2)}) copy-start(bf16[2,256,2048]{2,1,0:T(8,128)(2,1)} %panel.3) | copy-start | bytes 6291460
  58.7 1.0 copy-start.2
  59.8 0.8 copy-start.4
  60.6 0.8 copy-start.5
  61.5 21.2 %copy-start.1 = (bf16[2,256,2048]{2,1,0:T(8,128)(2,1)S(1)}, bf16[2,256,2048]{2,1,0:T(8,128)(2,1)}, u32[]{:S(2)}) copy-start(bf16[2,256,2048]{2,1,0:T(8,128)(2,1)} %panel.3) | copy-start | bytes 6291460

commit v2 on v1

v2 whole, which is shorter than its diff:
```python
import jax
import jax.numpy as jnp
from jax import lax
from jax.experimental import pallas as pl
from jax.experimental.pallas import tpu as pltpu
from jax.sharding import PartitionSpec as P

NO = 16
OO = NO * NO
R = 64
SLOTS = 16
LANES = 128
STEP = 0.25
BATCH = 4
TOLD = R // 2 + 8
SHIFT = 2.0**-12
TINY = 1e-30
HIGH = lax.Precision.HIGHEST
F32 = jnp.float32
BF16 = jnp.bfloat16


def dot(left, right, contract, precision=None):
    return lax.dot_general(
        left, right, (contract, ((), ())), precision=precision, preferred_element_type=F32
    )


def iota(shape, dim):
    return lax.broadcasted_iota(jnp.int32, shape, dim)


def pick_rows(ka_count, ta_count, told, sketch, bring):
    count = len(bring)

    def kernel(told, me, sketch_far, *refs):
        far, (picked, facts), near = refs[:count], refs[count : count + 2], refs[count + 2 :]
        near, (sketch, double, sem) = near[:count], near[count:]
        load = pltpu.make_async_copy(sketch_far, sketch, sem.at[count])
        load.start()
        loads = [pltpu.make_async_copy(far[i], near[i], sem.at[i]) for i in range(count)]
        for other in loads:
            other.start()
        begin = jnp.int32(0)
        length = jnp.int32(0)
        for place in range(ta_count):
            where_from, amount = told[place, 3], told[place, 2]
            begin = begin + jnp.where(where_from < me[0], amount, 0)
            length = length + jnp.where(where_from == me[0], amount, 0)
        facts[0] = begin
        facts[1] = length
        load.wait()
        for rank in range(sketch.shape[0]):
            rows = sketch[rank]
            double[rank] = jnp.concatenate([rows, rows], axis=1)
        left = iota(double.shape[1:], 1) < R

        def one(place, carry):
            picked[place] = jnp.where(left, double[told[place, 0]], double[told[place, 1]])
            return carry

        lax.fori_loop(0, ka_count, one, 0, unroll=8)
        for other in loads:
            other.wait()

    ranks, rows, _ = sketch.shape
    smem = pl.BlockSpec(memory_space=pltpu.SMEM)
    vmem = pl.BlockSpec(memory_space=pltpu.VMEM)
    hbm = pl.BlockSpec(memory_space=pltpu.HBM)
    me = lax.axis_index("ta").astype(jnp.int32).reshape(1)
    return pl.pallas_call(
        kernel,
        out_shape=(
            jax.ShapeDtypeStruct((ka_count, rows, LANES), BF16),
            jax.ShapeDtypeStruct((2,), jnp.int32),
        )
        + tuple(jax.ShapeDtypeStruct(x.shape, x.dtype) for x in bring),
        in_specs=[smem, smem] + [hbm] * (1 + count),
        out_specs=(vmem, smem) + (vmem,) * count,
        scratch_shapes=[
            pltpu.VMEM(sketch.shape, BF16),
            pltpu.VMEM((ranks, rows, LANES), BF16),
            pltpu.SemaphoreType.DMA((count + 1,)),
        ],
        compiler_params=pltpu.CompilerParams(vmem_limit_bytes=8 << 20),
        name="pick_rows",
    )(told, me, *[pltpu.with_memory_space_constraint(x, pltpu.HBM) for x in (sketch, *bring)])


def keep_mask(facts, rows, cols):
    slot = iota((rows, 1), 0) >> 4
    top = jnp.where(slot < facts[1], facts[0] + slot + SLOTS // 2, -1)
    group = iota((1, cols), 1) >> 4
    return group.astype(F32).astype(BF16) <= top.astype(F32).astype(BF16)


def inverse_factor(work, offset, down=True):
    for batch in range(0, R, BATCH):
        order = [c if down else R - 1 - c for c in range(batch, batch + BATCH)]
        edge = (order[0] // 8) * 8
        low, high = (edge, R) if down else (0, edge + 8)
        part = work[low:high]
        rows = high - low
        place = low + iota((rows, LANES), 0)
        columns = [
            jnp.broadcast_to(part[:, offset + c : offset + c + 1], (rows, LANES)) for c in order
        ]
        for step, pivot in enumerate(order):
            at = pivot - low
            column = columns[step]
            scale = 1.0 / column[at : at + 1]
            rest = jnp.where(place > pivot if down else place < pivot, column, 0.0)
            for later in range(step + 1, BATCH):
                columns[later] = columns[later] - rest * (columns[later][at : at + 1] * scale)
            part = part - rest * (part[at : at + 1] * scale)
        pieces = [work[:low]] * (low > 0) + [part] + [work[high:]] * (high < R)
        work = pieces[0] if len(pieces) == 1 else jnp.concatenate(pieces, axis=0)
    lane, row = iota((R, LANES), 1), iota((R, LANES), 0)
    diag = jnp.sum(jnp.where(lane == row + offset, work, 0.0), axis=1, keepdims=True)
    return work * lax.rsqrt(diag)


def factor_pair(gram, last_up):
    left = iota((R, LANES), 1) < R
    eye = unit()
    first = inverse_factor(jnp.where(left, gram, eye), 0)
    second = inverse_factor(jnp.where(left, eye, gram), R, down=not last_up)
    turned = pltpu.roll(second, R, 1)
    zero = jnp.zeros((R, LANES), F32)
    inverse = jnp.concatenate(
        [jnp.where(left, pltpu.roll(first, R, 1), zero), jnp.where(left, zero, turned)], axis=0
    )
    return first, turned, inverse


def unit():
    lane, row = iota((R, LANES), 1), iota((R, LANES), 0)
    return jnp.where((lane & (R - 1)) == row, 1.0, 0.0).astype(F32)


def grams(both):
    square = dot(both, both, ((0,), (0,)), HIGH)
    return jnp.where(iota((R, LANES), 1) < R, square[:R], square[R:])


def three_terms(value):
    high = value.astype(BF16)
    rest = value - high.astype(F32)
    middle = rest.astype(BF16)
    return [high, middle, (rest - middle.astype(F32)).astype(BF16)]


def sketch_panels(facts, chosen, panel, sigma, basis, coef, copies):
    def kernel(facts, chosen, far, sigma, basis, coef, sketched, shared, panel, sem):
        k_count, rows, cols = panel.shape
        loads = [pltpu.make_async_copy(far.at[k], panel.at[k], sem.at[k]) for k in range(k_count)]
        for load in loads:
            load.start()
        row, col = iota((OO, OO), 0), iota((OO, OO), 1)
        inner = (row & 15) == (col >> 4)
        spread = jnp.where((row & 15) == (col & 15), 1.0, 0.0).astype(F32)
        same = (row >> 4) == (col >> 4)
        lines = []
        for k in range(k_count):
            summed = dot(basis[...], sigma[k], ((1,), (0,)))
            pairs = dot(summed, coef[k].astype(F32), ((0,), (0,)), HIGH)
            laid = dot(jnp.where(inner, pairs, 0.0), spread, ((1,), (0,)), HIGH)
            line = jnp.sum(jnp.where(same, laid, 0.0), axis=0, keepdims=True)
            lines += [line[:, :LANES], line[:, LANES:]]

        keep = keep_mask(facts, rows, cols)
        zero = jnp.zeros((rows, cols), BF16)
        parts = []
        for k in range(k_count):
            loads[k].wait()
            masked = jnp.where(keep, panel[k], zero)
            panel[k] = masked
            parts.append(dot(masked, chosen[...], ((1,), (0,))))
        both = jnp.where(iota((rows, LANES), 1) < R, parts[0], parts[1])
        sketched[...] = both

        gram = grams(both)
        lane, row = iota((R, LANES), 1), iota((R, LANES), 0)
        left = lane < R
        trace = jnp.sum(gram * unit(), axis=0, keepdims=True)
        half = lane[:1] < R
        shift = jnp.where(
            half,
            jnp.sum(jnp.where(half, trace, 0.0), axis=1, keepdims=True),
            jnp.sum(jnp.where(half, 0.0, trace), axis=1, keepdims=True),
        )
        shift = shift * (SHIFT / R) + TINY
        first, second, inverse = factor_pair(gram + unit() * shift, True)
        corners = jnp.where(lane >= row, first, second)
        folded = jnp.where(left[: R // 2], corners[: R // 2], pltpu.roll(corners, R, 1)[R // 2 :])
        diag = jnp.sum(jnp.where(lane == row, second, 0.0), axis=0, keepdims=True)
        told = [folded, diag, shift] + lines + [jnp.zeros((2, LANES), F32)]
        told = jnp.concatenate(three_terms(jnp.concatenate(told, axis=0)), axis=0)
        own = dot(inverse, both, ((1,), (1,)), HIGH).astype(BF16)
        chunk = cols // copies
        halves = chunk // LANES
        for place in range(copies):
            shared[place, k_count * halves * R :] = told
        for k in range(k_count):
            terms = dot(own, panel[k], ((1,), (0,)))[k * R : (k + 1) * R].astype(BF16)
            for place in range(copies):
                for part in range(halves):
                    at = place * chunk + part * LANES
                    base = (k * halves + part) * R
                    shared[place, base : base + R] = terms[:, at : at + LANES]

    k_count, rows, cols = panel.shape
    smem = pl.BlockSpec(memory_space=pltpu.SMEM)
    vmem = pl.BlockSpec(memory_space=pltpu.VMEM)
    hbm = pl.BlockSpec(memory_space=pltpu.HBM)
    told_rows = k_count * R * (cols // copies // LANES) + 3 * TOLD
    return pl.pallas_call(
        kernel,
        out_shape=(
            jax.ShapeDtypeStruct((rows, LANES), F32),
            jax.ShapeDtypeStruct((copies, told_rows, LANES), BF16),
        ),
        in_specs=[smem, vmem, hbm, vmem, vmem, vmem],
        out_specs=(vmem, vmem),
        scratch_shapes=[pltpu.VMEM(panel.shape, BF16), pltpu.SemaphoreType.DMA((k_count,))],
        compiler_params=pltpu.CompilerParams(vmem_limit_bytes=20 << 20),
        name="sketch_panels",
    )(facts, chosen, pltpu.with_memory_space_constraint(panel, pltpu.HBM), sigma, basis, coef)


def finish_panels(told, sketched, green, hamilton, chunk):
    def kernel(told, sketched, green, hamilton, next_green, ortho, right):
        k_count, copies = green.shape[0], told.shape[0]
        halves = chunk // LANES
        top = k_count * halves * R
        lane, row = iota((R, LANES), 1), iota((R, LANES), 0)
        left = lane < R
        factors, extra = [], jnp.zeros((TOLD - R // 2, LANES), F32)
        for place in range(copies):
            high, middle, low = (
                told[place, top + i * TOLD : top + (i + 1) * TOLD].astype(F32) for i in range(3)
            )
            value = high + middle + low
            extra = extra + value[R // 2 :]
            corners = value[: R // 2]
            turned = pltpu.roll(corners, R, 1)
            diag = pltpu.roll(value[R // 2 : R // 2 + 1], R, 1)
            upper = jnp.concatenate([corners, turned], axis=0)
            lower = jnp.concatenate([turned, corners], axis=0)
            lower = jnp.where(
                lane - R < row, lower, jnp.where(lane - R == row, diag, jnp.zeros_like(lower))
            )
            factors.append(jnp.where(left, jnp.where(lane >= row, upper, 0.0), lower))
        factors = jnp.concatenate(factors, axis=0)
        _, _, inverse = factor_pair(grams(factors) - unit() * extra[1:2], False)

        first = factors.astype(BF16)
        second = (factors - first.astype(F32)).astype(BF16)
        sums = []
        for k in range(k_count):
            terms = [
                jnp.concatenate(
                    [
                        told[place, (k * halves + part) * R : (k * halves + part + 1) * R]
                        for place in range(copies)
                    ],
                    axis=0,
                )
                for part in range(halves)
            ]
            terms = jnp.concatenate(terms, axis=1)
            both = dot(first, terms, ((0,), (0,))) + dot(second, terms, ((0,), (0,)))
            sums.append(both[k * R : (k + 1) * R])
        coeffs = dot(inverse, jnp.concatenate(sums, axis=0), ((1,), (0,)), HIGH)
        turned = dot(inverse, sketched[...], ((1,), (1,)), HIGH)
        for k in range(k_count):
            right[k] = coeffs[k * R : (k + 1) * R]
            ortho[k] = turned[k * R : (k + 1) * R]

        outer = (iota((NO, OO), 1) >> 4) == iota((NO, OO), 0)
        tile = jnp.where((iota((NO, OO), 1) & 15) == iota((NO, OO), 0), 1.0, 0.0).astype(F32)

        def square(line):
            return dot(jnp.where(outer, line, 0.0), tile, ((1,), (1,)), HIGH)

        for k in range(k_count):
            base = 2 + 2 * k
            line = jnp.concatenate([extra[base : base + 1], extra[base + 1 : base + 2]], axis=1)
            rate = square(line) * (1.0 / 256.0)
            g, h = square(green[k : k + 1]), square(hamilton[k : k + 1])
            for _ in range(2):
                left_prod = dot(h, g, ((1,), (0,)), HIGH)
                right_prod = dot(g, h, ((1,), (0,)), HIGH)
                g = g + STEP * (left_prod - right_prod + rate)
            flat = jnp.where(outer, dot(g, tile, ((1,), (0,)), HIGH), 0.0)
            next_green[k : k + 1] = jnp.sum(flat, axis=0, keepdims=True)

    k_count, rows = green.shape[0], sketched.shape[0]
    vmem = pl.BlockSpec(memory_space=pltpu.VMEM)
    return pl.pallas_call(
        kernel,
        out_shape=(
            jax.ShapeDtypeStruct((k_count, OO), F32),
            jax.ShapeDtypeStruct((k_count, R, rows), F32),
            jax.ShapeDtypeStruct((k_count, R, chunk), F32),
        ),
        in_specs=[vmem] * 4,
        out_specs=(vmem, vmem, vmem),
        compiler_params=pltpu.CompilerParams(vmem_limit_bytes=20 << 20),
        name="finish_panels",
    )(told, sketched, green, hamilton)


def body(
    sigma_history,
    time_basis,
    history_coef,
    green_now,
    hamilton,
    panel_block,
    panel_lengths,
    owners,
    sketch,
):
    ka_count, ta_count = lax.axis_size("ka"), lax.axis_size("ta")
    k_count = green_now.shape[0]
    assert NO * sigma_history.shape[1] * ta_count == 65536 and k_count == 2
    groups = [
        [place * ta_count + (group + place) % ta_count for place in range(ka_count)]
        for group in range(ta_count)
    ]
    facts = jnp.concatenate(
        [owners[:, 0], panel_lengths, lax.axis_index("ta").astype(jnp.int32).reshape(1)]
    )
    facts = jnp.pad(facts, (0, LANES - 4))
    told = lax.all_to_all(
        jnp.broadcast_to(facts[None, None], (ka_count, 1, LANES)),
        ("ka", "ta"),
        0,
        0,
        axis_index_groups=groups,
    ).reshape(ka_count, LANES)
    bring = (sigma_history, time_basis.T, history_coef)
    picked, facts, sigma, basis, coef = pick_rows(ka_count, ta_count, told, sketch, bring)
    chosen = lax.all_to_all(picked, "ka", 0, 0).reshape(-1, LANES)
    sketched, shared = sketch_panels(facts, chosen, panel_block, sigma, basis, coef, ta_count)
    told = lax.all_to_all(shared, "ta", 0, 0)
    chunk = panel_block.shape[2] // ta_count
    green_next, ortho, right = finish_panels(told, sketched, green_now, hamilton, chunk)
    return (green_next, ortho.transpose(0, 2, 1), right)


def solution(mesh):
    in_specs = (
        P("ka", "ta", None),
        P("ta", None),
        P("ka", "ta", None),
        P("ka", None),
        P("ka", None),
        P("ka", "ta", None),
        P("ta"),
        P("ka", None),
        P(None, "ka", None),
    )
    out_specs = (P("ka", None), P("ka", "ta", None), P("ka", None, "ta"))
    return jax.shard_map(body, mesh=mesh, in_specs=in_specs, out_specs=out_specs, check_vma=False)
```

time: 113 us -> 98.1 us (0.87)
  blocking collectives: 90.1 us -> 80.2 us
  local copies, waits for them, and re-layouts: 5.28 us -> 0.03 us
    all_to_all x1 -> x0, blocking collectives: 20 us -> none  [body(): told = lax.all_to_all(terms, 'ta', 0, 0)]
    all_to_all x1, blocking collectives: 17.9 us -> 28.1 us  [body(): told = lax.all_to_all(shared, 'ta', 0, 0)]
    unnamed x16 -> x4, local copies, waits for them, and re-layouts: 5.25 us -> 0.01 us
    pallas_call x1, Pallas kernels: 8.68 us -> 4.97 us  [finish_panels(): pl.pallas_call(kernel, out_shape=(jax.ShapeDtypeStruct((k_count, OO), F32...]
    pallas_call x1, Pallas kernels: 3.25 us -> 6.91 us  [sketch_panels(): pl.pallas_call(kernel, out_shape=(jax.ShapeDtypeStruct((rows, LANES), F32...]
where the time goes in v2:
time: 98.1 us; the launch traced here: 97.1 us
  blocking collectives  80.2 us (82%)
  Pallas kernels  14.8 us (15%)
  between operations  1.3 us (1%)
    all_to_all x1, blocking collectives, body(): told = lax.all_to_all(shared, 'ta', 0, 0)  28.1 us
    all_to_all x1, blocking collectives, body(): lax.all_to_all(jnp.broadcast_to(facts[None, None], (ka_count, 1, LANES)),...  28 us
    all_to_all x1, blocking collectives, body(): chosen = lax.all_to_all(picked, 'ka', 0, 0).reshape(-1, LANES)  24.1 us
    pallas_call x1, Pallas kernels, sketch_panels(): pl.pallas_call(kernel, out_shape=(jax.ShapeDtypeStruct((rows, LANES), F32...  6.91 us
    pallas_call x1, Pallas kernels, finish_panels(): pl.pallas_call(kernel, out_shape=(jax.ShapeDtypeStruct((k_count, OO), F32...  4.97 us
    pallas_call x1, Pallas kernels, pick_rows(): pl.pallas_call(kernel, out_shape=(jax.ShapeDtypeStruct((ka_count, rows, L...  2.95 us

profile of v2, /device:TPU:6, one launch (start us, length us, event | category | flops | bytes accessed | tf_op | source)
XLA Modules:
  0.0 97.1 jit_solution(12602562393124423689)
XLA Ops:
  1.3 0.7 pad_add_fusion
  2.0 28.0 %all_to_all.15 = s32[64,1,128]{2,1,0:T(1,128)S(1)} all-to-all(s32[64,1,128]{2,1,0:T(1,128)S(1)} %broadcast_in_dim.2), channel_id=1, replica_groups={{0,9,18,27,36,45,54,63,64,73,82,91,100,109,118,127,128,137,146,155,164,..., dimensions={0} | all-to-all | bytes 65536 | tf_op jit(solution)/shard_map/all_to_all | solution.py:336
  30.1 2.9 %pick_rows.1 = (bf16[64,32,128]{2,1,0:T(8,128)(2,1)S(1)}, s32[2]{0:T(128)S(1)}, bf16[2,512,256]{2,1,0:T(8,128)(2,1)S(1)}, bf16[64,512]{1,0:T(8,128)(2,1)S(1)}, bf16[2,64,256]{2,1,0:T(8,128)(2,1)S(1)}) custom-call(s32[64,128]{1,0:T(8,128)S(1)} %bitcast.7, s32[1]{0:T(128)} %bitcast.1.me, bf16[16,32,64]{2,1,0:T(8,128)(2,1)} %sketch_far.1, ...), custom_call_target="tpu_custom_call" | custom-call | tf_op jit(solution)/shard_map/pick_rows/pallas_call | solution.py:71
  33.0 24.1 %all_to_all.16 = bf16[64,32,128]{2,1,0:T(8,128)(2,1)S(1)} all-to-all(bf16[64,32,128]{2,1,0:T(8,128)(2,1)S(1)} %get-tuple-element.14), channel_id=1, replica_groups=mesh['ka'=64,'ta'=8] {'ka'}, dimensions={0} | all-to-all | bytes 1048576 | tf_op jit(solution)/shard_map/all_to_all | solution.py:345
  57.1 0.0 copy-start
  57.1 0.0 copy-start.1
  57.1 6.9 %sketch_panels.1 = (f32[256,128]{1,0:T(8,128)S(1)}, bf16[8,376,128]{2,1,0:T(8,128)(2,1)S(1)}) custom-call(s32[2]{0:T(128)S(1)} %get-tuple-element.13.facts, bf16[2048,128]{1,0:T(8,128)(2,1)S(1)} %bitcast.6, bf16[2,256,2048]{2,1,0:T(8,128)(2,1)} %far.1, bf16[2,512,256]{2,1,0:T(8,128)(2,1)S(1)} %get-tuple-element.15.sigma, ...), custom_call_target="tpu_custom_call" | custom-call | tf_op jit(solution)/shard_map/sketch_panels/pallas_call | solution.py:217
  64.0 28.1 %all_to_all.17.told = bf16[8,376,128]{2,1,0:T(8,128)(2,1)S(1)} all-to-all(bf16[8,376,128]{2,1,0:T(8,128)(2,1)S(1)} %get-tuple-element.18), channel_id=1, replica_groups=mesh['ka'=64,'ta'=8] {'ta'}, dimensions={0} | all-to-all | bytes 1540096 | tf_op jit(solution)/shard_map/all_to_all | solution.py:347
  92.2 0.0 copy-done
  92.2 0.0 copy-done.1
  92.2 5.0 %finish_panels.1 = (f32[2,256]{1,0:T(2,128)}, f32[2,64,256]{2,1,0:T(8,128)}, f32[2,64,256]{2,1,0:T(8,128)}) custom-call(bf16[8,376,128]{2,1,0:T(8,128)(2,1)S(1)} %all_to_all.17.told, f32[256,128]{1,0:T(8,128)S(1)} %get-tuple-element.19.sketched, f32[2,256]{1,0:T(2,128)S(1)} %copy-done, f32[2,256]{1,0:T(2,128)S(1)} %copy-done.1), custom_call_target="tpu_custom_call" | custom-call | tf_op jit(solution)/shard_map/finish_panels/pallas_call | solution.py:300
  (2 shorter events, 0.0 us)
Async XLA Ops:
  57.1 35.0 %copy-start = (f32[2,256]{1,0:T(2,128)S(1)}, f32[2,256]{1,0:T(2,128)}, u32[]{:S(2)}) copy-start(f32[2,256]{1,0:T(2,128)} %green.1) | copy-start | bytes 6148
  57.1 35.0 %copy-start.1 = (f32[2,256]{1,0:T(2,128)S(1)}, f32[2,256]{1,0:T(2,128)}, u32[]{:S(2)}) copy-start(f32[2,256]{1,0:T(2,128)} %hamilton.1) | copy-start | bytes 6148

commit v3 on v2

--- a/solution.py
+++ b/solution.py
@@ -9,9 +9,10 @@
 OO = NO * NO
 R = 64
 SLOTS = 16
+TOTAL = 120
 LANES = 128
 STEP = 0.25
-BATCH = 4
+BATCH = 8
 TOLD = R // 2 + 8
 SHIFT = 2.0**-12
 TINY = 1e-30
@@ -20,6 +21,10 @@
 BF16 = jnp.bfloat16
 
 
+def turn(place):
+    return ((place >> 1) & 1) | ((place >> 3) & 2)
+
+
 def dot(left, right, contract, precision=None):
     return lax.dot_general(
         left, right, (contract, ((), ())), precision=precision, preferred_element_type=F32
@@ -30,24 +35,32 @@
     return lax.broadcasted_iota(jnp.int32, shape, dim)
 
 
-def pick_rows(ka_count, ta_count, told, sketch, bring):
+def pick_rows(ka_count, ta_count, told, me, sketch, bring):
     count = len(bring)
+    shapes = [x.shape for x in bring[:-1]] + [bring[-1].shape[1:]]
 
     def kernel(told, me, sketch_far, *refs):
         far, (picked, facts), near = refs[:count], refs[count : count + 2], refs[count + 2 :]
         near, (sketch, double, sem) = near[:count], near[count:]
         load = pltpu.make_async_copy(sketch_far, sketch, sem.at[count])
         load.start()
-        loads = [pltpu.make_async_copy(far[i], near[i], sem.at[i]) for i in range(count)]
+        loads = [
+            pltpu.make_async_copy(
+                far[i] if far[i].shape == near[i].shape else far[i].at[0], near[i], sem.at[i]
+            )
+            for i in range(count)
+        ]
         for other in loads:
             other.start()
-        begin = jnp.int32(0)
+        before = jnp.int32(0)
+        after = jnp.int32(0)
         length = jnp.int32(0)
-        for place in range(ta_count):
+        for place in (0, 2, 16, 18):
             where_from, amount = told[place, 3], told[place, 2]
-            begin = begin + jnp.where(where_from < me[0], amount, 0)
+            before = before + jnp.where(where_from < me[0], amount, 0)
+            after = after + jnp.where(where_from >= me[0], amount, 0)
             length = length + jnp.where(where_from == me[0], amount, 0)
-        facts[0] = begin
+        facts[0] = jnp.where(me[0] < ta_count // 2, before, TOTAL - after)
         facts[1] = length
         load.wait()
         for rank in range(sketch.shape[0]):
@@ -67,15 +80,14 @@
     smem = pl.BlockSpec(memory_space=pltpu.SMEM)
     vmem = pl.BlockSpec(memory_space=pltpu.VMEM)
     hbm = pl.BlockSpec(memory_space=pltpu.HBM)
-    me = lax.axis_index("ta").astype(jnp.int32).reshape(1)
     return pl.pallas_call(
         kernel,
         out_shape=(
             jax.ShapeDtypeStruct((ka_count, rows, LANES), BF16),
             jax.ShapeDtypeStruct((2,), jnp.int32),
         )
-        + tuple(jax.ShapeDtypeStruct(x.shape, x.dtype) for x in bring),
-        in_specs=[smem, smem] + [hbm] * (1 + count),
+        + tuple(jax.ShapeDtypeStruct(shape, x.dtype) for x, shape in zip(bring, shapes)),
+        in_specs=[smem] * 2 + [hbm] * (1 + count),
         out_specs=(vmem, smem) + (vmem,) * count,
         scratch_shapes=[
             pltpu.VMEM(sketch.shape, BF16),
@@ -133,6 +145,15 @@
     return first, turned, inverse
 
 
+def split_dot(left, right, contract):
+    (high, low), (top, rest) = (three_terms(x)[:2] for x in (left, right))
+    return dot(
+        jnp.concatenate([high, high, low], axis=contract[0][0]),
+        jnp.concatenate([top, rest, top], axis=contract[1][0]),
+        contract,
+    )
+
+
 def unit():
     lane, row = iota((R, LANES), 1), iota((R, LANES), 0)
     return jnp.where((lane & (R - 1)) == row, 1.0, 0.0).astype(F32)
@@ -150,30 +171,39 @@
     return [high, middle, (rest - middle.astype(F32)).astype(BF16)]
 
 
-def sketch_panels(facts, chosen, panel, sigma, basis, coef, copies):
-    def kernel(facts, chosen, far, sigma, basis, coef, sketched, shared, panel, sem):
+def sketch_panels(facts, chosen, panel, first_panel, sigma, basis, coef, copies):
+    def kernel(facts, chosen, far, near, sigma, basis, coef, sketched, shared, panel, sem):
         k_count, rows, cols = panel.shape
-        loads = [pltpu.make_async_copy(far.at[k], panel.at[k], sem.at[k]) for k in range(k_count)]
+        loads = [pltpu.make_async_copy(far.at[k], panel.at[k], sem.at[k]) for k in range(1, k_count)]
         for load in loads:
             load.start()
         row, col = iota((OO, OO), 0), iota((OO, OO), 1)
         inner = (row & 15) == (col >> 4)
-        spread = jnp.where((row & 15) == (col & 15), 1.0, 0.0).astype(F32)
-        same = (row >> 4) == (col >> 4)
+        spread = jnp.where((row & 15) == (col & 15), 1.0, 0.0).astype(BF16)
+        same = iota((NO, OO), 0) == (iota((NO, OO), 1) >> 4)
+        groups = []
+        for k in range(k_count):
+            summed = dot(basis[...], sigma[k], ((1,), (0,)))
+            summed = jnp.concatenate(three_terms(summed), axis=0)
+            pairs = dot(summed, jnp.concatenate([coef[k]] * 3, axis=0), ((0,), (0,)))
+            pairs = jnp.where(inner, pairs, 0.0).reshape(NO, NO, OO)
+            groups += three_terms(jnp.sum(pairs, axis=1))
+        laid = dot(jnp.concatenate(groups, axis=0), spread, ((1,), (0,)))
         lines = []
         for k in range(k_count):
-            summed = dot(basis[...], sigma[k], ((1,), (0,)))
-            pairs = dot(summed, coef[k].astype(F32), ((0,), (0,)), HIGH)
-            laid = dot(jnp.where(inner, pairs, 0.0), spread, ((1,), (0,)), HIGH)
-            line = jnp.sum(jnp.where(same, laid, 0.0), axis=0, keepdims=True)
+            base = 3 * NO * k
+            total = laid[base : base + NO] + laid[base + NO : base + 2 * NO]
+            total = total + laid[base + 2 * NO : base + 3 * NO]
+            line = jnp.sum(jnp.where(same, total, 0.0), axis=0, keepdims=True)
             lines += [line[:, :LANES], line[:, LANES:]]
 
         keep = keep_mask(facts, rows, cols)
         zero = jnp.zeros((rows, cols), BF16)
         parts = []
         for k in range(k_count):
-            loads[k].wait()
-            masked = jnp.where(keep, panel[k], zero)
+            if k > 0:
+                loads[k - 1].wait()
+            masked = jnp.where(keep, panel[k] if k > 0 else near[...], zero)
             panel[k] = masked
             parts.append(dot(masked, chosen[...], ((1,), (0,))))
         both = jnp.where(iota((rows, LANES), 1) < R, parts[0], parts[1])
@@ -195,8 +225,9 @@
         folded = jnp.where(left[: R // 2], corners[: R // 2], pltpu.roll(corners, R, 1)[R // 2 :])
         diag = jnp.sum(jnp.where(lane == row, second, 0.0), axis=0, keepdims=True)
         told = [folded, diag, shift] + lines + [jnp.zeros((2, LANES), F32)]
-        told = jnp.concatenate(three_terms(jnp.concatenate(told, axis=0)), axis=0)
-        own = dot(inverse, both, ((1,), (1,)), HIGH).astype(BF16)
+        told = three_terms(jnp.concatenate(told, axis=0))
+        told = jnp.concatenate(told + [jnp.zeros((128 - 3 * TOLD, LANES), BF16)], axis=0)
+        own = split_dot(inverse, both, ((1,), (1,))).astype(BF16)
         chunk = cols // copies
         halves = chunk // LANES
         for place in range(copies):
@@ -213,19 +244,27 @@
     smem = pl.BlockSpec(memory_space=pltpu.SMEM)
     vmem = pl.BlockSpec(memory_space=pltpu.VMEM)
     hbm = pl.BlockSpec(memory_space=pltpu.HBM)
-    told_rows = k_count * R * (cols // copies // LANES) + 3 * TOLD
+    told_rows = k_count * R * (cols // copies // LANES) + 128
     return pl.pallas_call(
         kernel,
         out_shape=(
             jax.ShapeDtypeStruct((rows, LANES), F32),
             jax.ShapeDtypeStruct((copies, told_rows, LANES), BF16),
         ),
-        in_specs=[smem, vmem, hbm, vmem, vmem, vmem],
+        in_specs=[smem, vmem, hbm, vmem, vmem, vmem, vmem],
         out_specs=(vmem, vmem),
         scratch_shapes=[pltpu.VMEM(panel.shape, BF16), pltpu.SemaphoreType.DMA((k_count,))],
         compiler_params=pltpu.CompilerParams(vmem_limit_bytes=20 << 20),
         name="sketch_panels",
-    )(facts, chosen, pltpu.with_memory_space_constraint(panel, pltpu.HBM), sigma, basis, coef)
+    )(
+        facts,
+        chosen,
+        pltpu.with_memory_space_constraint(panel, pltpu.HBM),
+        first_panel,
+        sigma,
+        basis,
+        coef,
+    )
 
 
 def finish_panels(told, sketched, green, hamilton, chunk):
@@ -251,6 +290,24 @@
                 lane - R < row, lower, jnp.where(lane - R == row, diag, jnp.zeros_like(lower))
             )
             factors.append(jnp.where(left, jnp.where(lane >= row, upper, 0.0), lower))
+        outer = (iota((NO, OO), 1) >> 4) == iota((NO, OO), 0)
+        tile = jnp.where((iota((NO, OO), 1) & 15) == iota((NO, OO), 0), 1.0, 0.0).astype(F32)
+
+        def square(line):
+            return dot(jnp.where(outer, line, 0.0), tile, ((1,), (1,)), HIGH)
+
+        for k in range(k_count):
+            base = 2 + 2 * k
+            line = jnp.concatenate([extra[base : base + 1], extra[base + 1 : base + 2]], axis=1)
+            rate = square(line) * (1.0 / 256.0)
+            g, h = square(green[k : k + 1]), square(hamilton[k : k + 1])
+            for _ in range(2):
+                left_prod = dot(h, g, ((1,), (0,)), HIGH)
+                right_prod = dot(g, h, ((1,), (0,)), HIGH)
+                g = g + STEP * (left_prod - right_prod + rate)
+            flat = jnp.where(outer, dot(g, tile, ((1,), (0,)), HIGH), 0.0)
+            next_green[k : k + 1] = jnp.sum(flat, axis=0, keepdims=True)
+
         factors = jnp.concatenate(factors, axis=0)
         _, _, inverse = factor_pair(grams(factors) - unit() * extra[1:2], False)
 
@@ -271,29 +328,11 @@
             terms = jnp.concatenate(terms, axis=1)
             both = dot(first, terms, ((0,), (0,))) + dot(second, terms, ((0,), (0,)))
             sums.append(both[k * R : (k + 1) * R])
-        coeffs = dot(inverse, jnp.concatenate(sums, axis=0), ((1,), (0,)), HIGH)
-        turned = dot(inverse, sketched[...], ((1,), (1,)), HIGH)
+        coeffs = split_dot(inverse, jnp.concatenate(sums, axis=0), ((1,), (0,)))
+        turned = split_dot(inverse, sketched[...], ((1,), (1,)))
         for k in range(k_count):
             right[k] = coeffs[k * R : (k + 1) * R]
             ortho[k] = turned[k * R : (k + 1) * R]
-
-        outer = (iota((NO, OO), 1) >> 4) == iota((NO, OO), 0)
-        tile = jnp.where((iota((NO, OO), 1) & 15) == iota((NO, OO), 0), 1.0, 0.0).astype(F32)
-
-        def square(line):
-            return dot(jnp.where(outer, line, 0.0), tile, ((1,), (1,)), HIGH)
-
-        for k in range(k_count):
-            base = 2 + 2 * k
-            line = jnp.concatenate([extra[base : base + 1], extra[base + 1 : base + 2]], axis=1)
-            rate = square(line) * (1.0 / 256.0)
-            g, h = square(green[k : k + 1]), square(hamilton[k : k + 1])
-            for _ in range(2):
-                left_prod = dot(h, g, ((1,), (0,)), HIGH)
-                right_prod = dot(g, h, ((1,), (0,)), HIGH)
-                g = g + STEP * (left_prod - right_prod + rate)
-            flat = jnp.where(outer, dot(g, tile, ((1,), (0,)), HIGH), 0.0)
-            next_green[k : k + 1] = jnp.sum(flat, axis=0, keepdims=True)
 
     k_count, rows = green.shape[0], sketched.shape[0]
     vmem = pl.BlockSpec(memory_space=pltpu.VMEM)
@@ -326,24 +365,29 @@
     k_count = green_now.shape[0]
     assert NO * sigma_history.shape[1] * ta_count == 65536 and k_count == 2
     groups = [
-        [place * ta_count + (group + place) % ta_count for place in range(ka_count)]
+        [place * ta_count + (group ^ turn(place)) for place in range(ka_count)]
         for group in range(ta_count)
     ]
-    facts = jnp.concatenate(
-        [owners[:, 0], panel_lengths, lax.axis_index("ta").astype(jnp.int32).reshape(1)]
-    )
-    facts = jnp.pad(facts, (0, LANES - 4))
+    me = lax.axis_index("ta").astype(jnp.int32).reshape(1)
+    asked = jnp.pad(owners.reshape(1, 2), ((0, 0), (0, LANES - 2)))
+    asked = asked + jnp.pad(panel_lengths[None], ((0, 0), (2, LANES - 3)))
+    asked = asked + jnp.where(iota((1, LANES), 1) == 3, me[0], 0)
+    asked = jnp.broadcast_to(asked[None], (ka_count, 1, LANES))
     told = lax.all_to_all(
-        jnp.broadcast_to(facts[None, None], (ka_count, 1, LANES)),
+        asked,
         ("ka", "ta"),
         0,
         0,
         axis_index_groups=groups,
     ).reshape(ka_count, LANES)
-    bring = (sigma_history, time_basis.T, history_coef)
-    picked, facts, sigma, basis, coef = pick_rows(ka_count, ta_count, told, sketch, bring)
+    bring = (sigma_history, time_basis.T, history_coef, panel_block)
+    picked, facts, sigma, basis, coef, panel = pick_rows(
+        ka_count, ta_count, told, me, sketch, bring
+    )
     chosen = lax.all_to_all(picked, "ka", 0, 0).reshape(-1, LANES)
-    sketched, shared = sketch_panels(facts, chosen, panel_block, sigma, basis, coef, ta_count)
+    sketched, shared = sketch_panels(
+        facts, chosen, panel_block, panel, sigma, basis, coef, ta_count
+    )
     told = lax.all_to_all(shared, "ta", 0, 0)
     chunk = panel_block.shape[2] // ta_count
     green_next, ortho, right = finish_panels(told, sketched, green_now, hamilton, chunk)

time: 98.1 us -> 94 us (0.958)
  Pallas kernels: 14.8 us -> 12.3 us
  blocking collectives: 80.2 us -> 78.7 us
    all_to_all x1, blocking collectives: 28 us -> 22.8 us  [body(): lax.all_to_all(asked, ('ka', 'ta'), 0, 0, axis_index_groups=groups)]
    all_to_all x1, blocking collectives: 28.1 us -> 31.3 us  [body(): told = lax.all_to_all(shared, 'ta', 0, 0)]
    pallas_call x1, Pallas kernels: 6.91 us -> 4.91 us  [sketch_panels(): pl.pallas_call(kernel, out_shape=(jax.ShapeDtypeStruct((rows, LANES), F32...]
where the time goes in v3:
time: 94 us; the launch traced here: 93.1 us
  blocking collectives  78.7 us (84%)
  Pallas kernels  12.3 us (13%)
  between operations  1.3 us (1%)
    all_to_all x1, blocking collectives, body(): told = lax.all_to_all(shared, 'ta', 0, 0)  31.3 us
    all_to_all x1, blocking collectives, body(): chosen = lax.all_to_all(picked, 'ka', 0, 0).reshape(-1, LANES)  24.6 us
    all_to_all x1, blocking collectives, body(): lax.all_to_all(asked, ('ka', 'ta'), 0, 0, axis_index_groups=groups)  22.8 us
    pallas_call x1, Pallas kernels, sketch_panels(): pl.pallas_call(kernel, out_shape=(jax.ShapeDtypeStruct((rows, LANES), F32...  4.91 us
    pallas_call x1, Pallas kernels, finish_panels(): pl.pallas_call(kernel, out_shape=(jax.ShapeDtypeStruct((k_count, OO), F32...  4.21 us
    pallas_call x1, Pallas kernels, pick_rows(): pl.pallas_call(kernel, out_shape=(jax.ShapeDtypeStruct((ka_count, rows, L...  3.21 us

profile of v3, /device:TPU:6, one launch (start us, length us, event | category | flops | bytes accessed | tf_op | source)
XLA Modules:
  0.0 93.1 jit_solution(13121545914806026729)
XLA Ops:
  1.3 0.7 fusion.1
  2.0 22.8 %all_to_all.15 = s32[64,1,128]{2,1,0:T(1,128)S(1)} all-to-all(s32[64,1,128]{2,1,0:T(1,128)S(1)} %broadcast_in_dim.23), channel_id=1, replica_groups={{0,8,17,25,32,40,49,57,64,72,81,89,96,104,113,121,130,138,147,155,162,1..., dimensions={0} | all-to-all | bytes 65536 | tf_op jit(solution)/shard_map/all_to_all | solution.py:376
  24.8 3.2 %pick_rows.1 = (bf16[64,32,128]{2,1,0:T(8,128)(2,1)S(1)}, s32[2]{0:T(128)S(1)}, bf16[2,512,256]{2,1,0:T(8,128)(2,1)S(1)}, bf16[64,512]{1,0:T(8,128)(2,1)S(1)}, b...) custom-call(s32[64,128]{1,0:T(8,128)S(1)} %bitcast.11, s32[1]{0:T(128)} %bitcast.4.me, ...), custom_call_target="tpu_custom_call" | custom-call | tf_op jit(solution)/shard_map/pick_rows/pallas_call | solution.py:83
  28.1 24.6 %all_to_all.16 = bf16[64,32,128]{2,1,0:T(8,128)(2,1)S(1)} all-to-all(bf16[64,32,128]{2,1,0:T(8,128)(2,1)S(1)} %get-tuple-element.15), channel_id=1, replica_groups=mesh['ka'=64,'ta'=8] {'ka'}, dimensions={0} | all-to-all | bytes 1048576 | tf_op jit(solution)/shard_map/all_to_all | solution.py:387
  52.7 0.0 copy-start
  52.7 0.0 copy-start.1
  52.7 4.9 %sketch_panels.1 = (f32[256,128]{1,0:T(8,128)S(1)}, bf16[8,384,128]{2,1,0:T(8,128)(2,1)S(1)}) custom-call(s32[2]{0:T(128)S(1)} %get-tuple-element.14.facts, bf16[2048,128]{1,0:T(8,128)(2,1)S(1)} %bitcast.10, bf16[2,256,2048]{2,1,0:T(8,128)(2,1)} %far.1, bf16[256,2048]{1,0:T(8,128)(2,1)S(1)} %get-tuple-element.16.near, ...), custom_call_target="tpu_custom_call" | custom-call | tf_op jit(solution)/shard_map/sketch_panels/pallas_call | solution.py:248
  57.6 31.3 %all_to_all.17.told = bf16[8,384,128]{2,1,0:T(8,128)(2,1)S(1)} all-to-all(bf16[8,384,128]{2,1,0:T(8,128)(2,1)S(1)} %get-tuple-element.20), channel_id=1, replica_groups=mesh['ka'=64,'ta'=8] {'ta'}, dimensions={0} | all-to-all | bytes 1572864 | tf_op jit(solution)/shard_map/all_to_all | solution.py:391
  88.9 0.0 copy-done
  88.9 0.0 copy-done.1
  88.9 4.2 %finish_panels.1 = (f32[2,256]{1,0:T(2,128)}, f32[2,64,256]{2,1,0:T(8,128)}, f32[2,64,256]{2,1,0:T(8,128)}) custom-call(bf16[8,384,128]{2,1,0:T(8,128)(2,1)S(1)} %all_to_all.17.told, f32[256,128]{1,0:T(8,128)S(1)} %get-tuple-element.21.sketched, f32[2,256]{1,0:T(2,128)S(1)} %copy-done, f32[2,256]{1,0:T(2,128)S(1)} %copy-done.1), custom_call_target="tpu_custom_call" | custom-call | tf_op jit(solution)/shard_map/finish_panels/pallas_call | solution.py:339
  (1 shorter events, 0.0 us)
Async XLA Ops:
  52.7 36.2 %copy-start = (f32[2,256]{1,0:T(2,128)S(1)}, f32[2,256]{1,0:T(2,128)}, u32[]{:S(2)}) copy-start(f32[2,256]{1,0:T(2,128)} %green.1) | copy-start | bytes 6148
  52.7 36.2 %copy-start.1 = (f32[2,256]{1,0:T(2,128)S(1)}, f32[2,256]{1,0:T(2,128)}, u32[]{:S(2)}) copy-start(f32[2,256]{1,0:T(2,128)} %hamilton.1) | copy-start | bytes 6148

commit v4 on v3

--- a/solution.py
+++ b/solution.py
@@ -37,19 +37,13 @@
 
 def pick_rows(ka_count, ta_count, told, me, sketch, bring):
     count = len(bring)
-    shapes = [x.shape for x in bring[:-1]] + [bring[-1].shape[1:]]
 
     def kernel(told, me, sketch_far, *refs):
         far, (picked, facts), near = refs[:count], refs[count : count + 2], refs[count + 2 :]
         near, (sketch, double, sem) = near[:count], near[count:]
         load = pltpu.make_async_copy(sketch_far, sketch, sem.at[count])
         load.start()
-        loads = [
-            pltpu.make_async_copy(
-                far[i] if far[i].shape == near[i].shape else far[i].at[0], near[i], sem.at[i]
-            )
-            for i in range(count)
-        ]
+        loads = [pltpu.make_async_copy(far[i], near[i], sem.at[i]) for i in range(count)]
         for other in loads:
             other.start()
         before = jnp.int32(0)
@@ -86,7 +80,7 @@
             jax.ShapeDtypeStruct((ka_count, rows, LANES), BF16),
             jax.ShapeDtypeStruct((2,), jnp.int32),
         )
-        + tuple(jax.ShapeDtypeStruct(shape, x.dtype) for x, shape in zip(bring, shapes)),
+        + tuple(jax.ShapeDtypeStruct(x.shape, x.dtype) for x in bring),
         in_specs=[smem] * 2 + [hbm] * (1 + count),
         out_specs=(vmem, smem) + (vmem,) * count,
         scratch_shapes=[
@@ -104,6 +98,18 @@
     top = jnp.where(slot < facts[1], facts[0] + slot + SLOTS // 2, -1)
     group = iota((1, cols), 1) >> 4
     return group.astype(F32).astype(BF16) <= top.astype(F32).astype(BF16)
+
+
+def together(*stages):
+    results, running = {}, dict(enumerate(stages))
+    while running:
+        for place, stage in list(running.items()):
+            try:
+                next(stage)
+            except StopIteration as end:
+                results[place] = end.value
+                del running[place]
+    return [results[place] for place in range(len(stages))]
 
 
 def inverse_factor(work, offset, down=True):
@@ -127,22 +133,70 @@
             part = part - rest * (part[at : at + 1] * scale)
         pieces = [work[:low]] * (low > 0) + [part] + [work[high:]] * (high < R)
         work = pieces[0] if len(pieces) == 1 else jnp.concatenate(pieces, axis=0)
+        yield
     lane, row = iota((R, LANES), 1), iota((R, LANES), 0)
     diag = jnp.sum(jnp.where(lane == row + offset, work, 0.0), axis=1, keepdims=True)
     return work * lax.rsqrt(diag)
 
 
-def factor_pair(gram, last_up):
+def inverse_pair(work):
+    width = 8
+    spot = iota((R, LANES), 1) & (R - 1)
+    row, left = iota((R, LANES), 0), iota((R, LANES), 1) < R
+    one, own_row = spot[:1], row[:width]
+    for start in range(0, R, width):
+        top, rest = work[start : start + width], work[start + width :]
+        part = work[start:]
+        columns = [
+            jnp.where(
+                left[start:],
+                jnp.broadcast_to(part[:, c : c + 1], part.shape),
+                jnp.broadcast_to(part[:, R + c : R + c + 1], part.shape),
+            )
+            for c in range(start, start + width)
+        ]
+        inside = (one >= start) & (one < start + width)
+        rest = jnp.where(inside, 0.0, rest)
+        for step in range(width):
+            pivot = start + step
+            column = columns[step]
+            scale = 1.0 / column[step : step + 1]
+            upper = jnp.where(own_row > step, column[:width], 0.0)
+            column = jnp.concatenate([upper, column[width:]], axis=0) if start + width < R else upper
+            for later in range(step + 1, width):
+                columns[later] = columns[later] - column * (columns[later][step : step + 1] * scale)
+            line = jnp.where(one == pivot, 1.0, top[step : step + 1]) * scale
+            gone = (spot[:width] == pivot) & (own_row > step)
+            top = jnp.where(gone, 0.0, top) - upper * line
+            if start + width < R:
+                rest = rest - column[width:] * jnp.where(inside & (one > pivot), 0.0, line)
+        pieces = [work[:start]] * (start > 0) + [top] + [rest] * (start + width < R)
+        work = jnp.concatenate(pieces, axis=0)
+        yield
+    diag = jnp.where(spot == row, work, 0.0)
+    scale = jnp.where(
+        left,
+        lax.rsqrt(jnp.sum(jnp.where(left, diag, 0.0), axis=1, keepdims=True)),
+        lax.rsqrt(jnp.sum(jnp.where(left, 0.0, diag), axis=1, keepdims=True)),
+    )
+    work = jnp.where(spot < row, work * scale, jnp.where(spot == row, scale, 0.0))
+    return jnp.concatenate([jnp.where(left, work, 0.0), jnp.where(left, 0.0, work)], axis=0)
+
+
+def factor_pair(gram, beside):
     left = iota((R, LANES), 1) < R
     eye = unit()
-    first = inverse_factor(jnp.where(left, gram, eye), 0)
-    second = inverse_factor(jnp.where(left, eye, gram), R, down=not last_up)
+    first, second, other = together(
+        inverse_factor(jnp.where(left, gram, eye), 0),
+        inverse_factor(jnp.where(left, eye, gram), R, down=False),
+        beside,
+    )
     turned = pltpu.roll(second, R, 1)
     zero = jnp.zeros((R, LANES), F32)
     inverse = jnp.concatenate(
         [jnp.where(left, pltpu.roll(first, R, 1), zero), jnp.where(left, zero, turned)], axis=0
     )
-    return first, turned, inverse
+    return first, turned, inverse, other
 
 
 def split_dot(left, right, contract):
@@ -171,39 +225,41 @@
     return [high, middle, (rest - middle.astype(F32)).astype(BF16)]
 
 
-def sketch_panels(facts, chosen, panel, first_panel, sigma, basis, coef, copies):
-    def kernel(facts, chosen, far, near, sigma, basis, coef, sketched, shared, panel, sem):
+def sketch_panels(facts, chosen, panel, sigma, basis, coef, copies):
+    def kernel(facts, chosen, near, sigma, basis, coef, sketched, shared, panel):
         k_count, rows, cols = panel.shape
-        loads = [pltpu.make_async_copy(far.at[k], panel.at[k], sem.at[k]) for k in range(1, k_count)]
-        for load in loads:
-            load.start()
-        row, col = iota((OO, OO), 0), iota((OO, OO), 1)
-        inner = (row & 15) == (col >> 4)
-        spread = jnp.where((row & 15) == (col & 15), 1.0, 0.0).astype(BF16)
-        same = iota((NO, OO), 0) == (iota((NO, OO), 1) >> 4)
-        groups = []
-        for k in range(k_count):
-            summed = dot(basis[...], sigma[k], ((1,), (0,)))
-            summed = jnp.concatenate(three_terms(summed), axis=0)
-            pairs = dot(summed, jnp.concatenate([coef[k]] * 3, axis=0), ((0,), (0,)))
-            pairs = jnp.where(inner, pairs, 0.0).reshape(NO, NO, OO)
-            groups += three_terms(jnp.sum(pairs, axis=1))
-        laid = dot(jnp.concatenate(groups, axis=0), spread, ((1,), (0,)))
-        lines = []
-        for k in range(k_count):
-            base = 3 * NO * k
-            total = laid[base : base + NO] + laid[base + NO : base + 2 * NO]
-            total = total + laid[base + 2 * NO : base + 3 * NO]
-            line = jnp.sum(jnp.where(same, total, 0.0), axis=0, keepdims=True)
-            lines += [line[:, :LANES], line[:, LANES:]]
+
+        def history():
+            row, col = iota((OO, OO), 0), iota((OO, OO), 1)
+            inner = (row & 15) == (col >> 4)
+            spread = jnp.where((row & 15) == (col & 15), 1.0, 0.0).astype(BF16)
+            same = iota((NO, OO), 0) == (iota((NO, OO), 1) >> 4)
+            groups = []
+            for k in range(k_count):
+                summed = dot(basis[...], sigma[k], ((1,), (0,)))
+                yield
+                summed = jnp.concatenate(three_terms(summed), axis=0)
+                pairs = dot(summed, jnp.concatenate([coef[k]] * 3, axis=0), ((0,), (0,)))
+                yield
+                pairs = jnp.where(inner, pairs, 0.0).reshape(NO, NO, OO)
+                groups += three_terms(jnp.sum(pairs, axis=1))
+                yield
+            laid = dot(jnp.concatenate(groups, axis=0), spread, ((1,), (0,)))
+            yield
+            lines = []
+            for k in range(k_count):
+                base = 3 * NO * k
+                total = laid[base : base + NO] + laid[base + NO : base + 2 * NO]
+                total = total + laid[base + 2 * NO : base + 3 * NO]
+                line = jnp.sum(jnp.where(same, total, 0.0), axis=0, keepdims=True)
+                lines += [line[:, :LANES], line[:, LANES:]]
+            return lines
 
         keep = keep_mask(facts, rows, cols)
         zero = jnp.zeros((rows, cols), BF16)
         parts = []
         for k in range(k_count):
-            if k > 0:
-                loads[k - 1].wait()
-            masked = jnp.where(keep, panel[k] if k > 0 else near[...], zero)
+            masked = jnp.where(keep, near[k], zero)
             panel[k] = masked
             parts.append(dot(masked, chosen[...], ((1,), (0,))))
         both = jnp.where(iota((rows, LANES), 1) < R, parts[0], parts[1])
@@ -220,7 +276,7 @@
             jnp.sum(jnp.where(half, 0.0, trace), axis=1, keepdims=True),
         )
         shift = shift * (SHIFT / R) + TINY
-        first, second, inverse = factor_pair(gram + unit() * shift, True)
+        first, second, inverse, lines = factor_pair(gram + unit() * shift, history())
         corners = jnp.where(lane >= row, first, second)
         folded = jnp.where(left[: R // 2], corners[: R // 2], pltpu.roll(corners, R, 1)[R // 2 :])
         diag = jnp.sum(jnp.where(lane == row, second, 0.0), axis=0, keepdims=True)
@@ -243,7 +299,6 @@
     k_count, rows, cols = panel.shape
     smem = pl.BlockSpec(memory_space=pltpu.SMEM)
     vmem = pl.BlockSpec(memory_space=pltpu.VMEM)
-    hbm = pl.BlockSpec(memory_space=pltpu.HBM)
     told_rows = k_count * R * (cols // copies // LANES) + 128
     return pl.pallas_call(
         kernel,
@@ -251,20 +306,12 @@
             jax.ShapeDtypeStruct((rows, LANES), F32),
             jax.ShapeDtypeStruct((copies, told_rows, LANES), BF16),
         ),
-        in_specs=[smem, vmem, hbm, vmem, vmem, vmem, vmem],
+        in_specs=[smem] + [vmem] * 5,
         out_specs=(vmem, vmem),
-        scratch_shapes=[pltpu.VMEM(panel.shape, BF16), pltpu.SemaphoreType.DMA((k_count,))],
+        scratch_shapes=[pltpu.VMEM(panel.shape, BF16)],
         compiler_params=pltpu.CompilerParams(vmem_limit_bytes=20 << 20),
         name="sketch_panels",
-    )(
-        facts,
-        chosen,
-        pltpu.with_memory_space_constraint(panel, pltpu.HBM),
-        first_panel,
-        sigma,
-        basis,
-        coef,
-    )
+    )(facts, chosen, panel, sigma, basis, coef)
 
 
 def finish_panels(told, sketched, green, hamilton, chunk):
@@ -290,45 +337,61 @@
                 lane - R < row, lower, jnp.where(lane - R == row, diag, jnp.zeros_like(lower))
             )
             factors.append(jnp.where(left, jnp.where(lane >= row, upper, 0.0), lower))
-        outer = (iota((NO, OO), 1) >> 4) == iota((NO, OO), 0)
-        tile = jnp.where((iota((NO, OO), 1) & 15) == iota((NO, OO), 0), 1.0, 0.0).astype(F32)
-
-        def square(line):
-            return dot(jnp.where(outer, line, 0.0), tile, ((1,), (1,)), HIGH)
-
-        for k in range(k_count):
-            base = 2 + 2 * k
-            line = jnp.concatenate([extra[base : base + 1], extra[base + 1 : base + 2]], axis=1)
-            rate = square(line) * (1.0 / 256.0)
-            g, h = square(green[k : k + 1]), square(hamilton[k : k + 1])
+        factors = jnp.concatenate(factors, axis=0)
+
+        def beside():
+            outer = (iota((NO, OO), 1) >> 4) == iota((NO, OO), 0)
+            tile = jnp.where((iota((NO, OO), 1) & 15) == iota((NO, OO), 0), 1.0, 0.0).astype(F32)
+
+            def square(line):
+                return dot(jnp.where(outer, line, 0.0), tile, ((1,), (1,)), HIGH)
+
+            rates = []
+            for k in range(k_count):
+                base = 2 + 2 * k
+                line = jnp.concatenate([extra[base : base + 1], extra[base + 1 : base + 2]], axis=1)
+                rates.append(square(line) * (1.0 / 256.0))
+            states = [square(green[k : k + 1]) for k in range(k_count)]
+            operators = [square(hamilton[k : k + 1]) for k in range(k_count)]
+            yield
             for _ in range(2):
-                left_prod = dot(h, g, ((1,), (0,)), HIGH)
-                right_prod = dot(g, h, ((1,), (0,)), HIGH)
-                g = g + STEP * (left_prod - right_prod + rate)
-            flat = jnp.where(outer, dot(g, tile, ((1,), (0,)), HIGH), 0.0)
-            next_green[k : k + 1] = jnp.sum(flat, axis=0, keepdims=True)
-
-        factors = jnp.concatenate(factors, axis=0)
-        _, _, inverse = factor_pair(grams(factors) - unit() * extra[1:2], False)
-
-        first = factors.astype(BF16)
-        second = (factors - first.astype(F32)).astype(BF16)
-        sums = []
-        for k in range(k_count):
-            terms = [
-                jnp.concatenate(
-                    [
-                        told[place, (k * halves + part) * R : (k * halves + part + 1) * R]
-                        for place in range(copies)
-                    ],
-                    axis=0,
-                )
-                for part in range(halves)
-            ]
-            terms = jnp.concatenate(terms, axis=1)
-            both = dot(first, terms, ((0,), (0,))) + dot(second, terms, ((0,), (0,)))
-            sums.append(both[k * R : (k + 1) * R])
-        coeffs = split_dot(inverse, jnp.concatenate(sums, axis=0), ((1,), (0,)))
+                pairs = [
+                    (dot(h, g, ((1,), (0,)), HIGH), dot(g, h, ((1,), (0,)), HIGH))
+                    for g, h in zip(states, operators)
+                ]
+                states = [
+                    g + STEP * (left_prod - right_prod + rate)
+                    for g, (left_prod, right_prod), rate in zip(states, pairs, rates)
+                ]
+                yield
+            for k in range(k_count):
+                flat = jnp.where(outer, dot(states[k], tile, ((1,), (0,)), HIGH), 0.0)
+                next_green[k : k + 1] = jnp.sum(flat, axis=0, keepdims=True)
+            yield
+            first = factors.astype(BF16)
+            second = (factors - first.astype(F32)).astype(BF16)
+            sums = []
+            for k in range(k_count):
+                terms = [
+                    jnp.concatenate(
+                        [
+                            told[place, (k * halves + part) * R : (k * halves + part + 1) * R]
+                            for place in range(copies)
+                        ],
+                        axis=0,
+                    )
+                    for part in range(halves)
+                ]
+                terms = jnp.concatenate(terms, axis=1)
+                both = dot(first, terms, ((0,), (0,))) + dot(second, terms, ((0,), (0,)))
+                sums.append(both[k * R : (k + 1) * R])
+                yield
+            return jnp.concatenate(sums, axis=0)
+
+        inverse, sums = together(
+            inverse_pair(grams(factors) - unit() * extra[1:2]), beside()
+        )
+        coeffs = split_dot(inverse, sums, ((1,), (0,)))
         turned = split_dot(inverse, sketched[...], ((1,), (1,)))
         for k in range(k_count):
             right[k] = coeffs[k * R : (k + 1) * R]
@@ -369,10 +432,9 @@
         for group in range(ta_count)
     ]
     me = lax.axis_index("ta").astype(jnp.int32).reshape(1)
-    asked = jnp.pad(owners.reshape(1, 2), ((0, 0), (0, LANES - 2)))
-    asked = asked + jnp.pad(panel_lengths[None], ((0, 0), (2, LANES - 3)))
-    asked = asked + jnp.where(iota((1, LANES), 1) == 3, me[0], 0)
-    asked = jnp.broadcast_to(asked[None], (ka_count, 1, LANES))
+    asked = jnp.pad(owners.reshape(2), (0, LANES - 2)) + jnp.pad(panel_lengths, (2, LANES - 3))
+    asked = asked + jnp.where(iota((1, LANES), 1)[0] == 3, me[0], 0)
+    asked = jnp.broadcast_to(asked[None, None], (ka_count, 1, LANES))
     told = lax.all_to_all(
         asked,
         ("ka", "ta"),
@@ -385,9 +447,7 @@
         ka_count, ta_count, told, me, sketch, bring
     )
     chosen = lax.all_to_all(picked, "ka", 0, 0).reshape(-1, LANES)
-    sketched, shared = sketch_panels(
-        facts, chosen, panel_block, panel, sigma, basis, coef, ta_count
-    )
+    sketched, shared = sketch_panels(facts, chosen, panel, sigma, basis, coef, ta_count)
     told = lax.all_to_all(shared, "ta", 0, 0)
     chunk = panel_block.shape[2] // ta_count
     green_next, ortho, right = finish_panels(told, sketched, green_now, hamilton, chunk)

time: 94 us -> 92.6 us (0.985)
  Pallas kernels: 12.3 us -> 10.9 us
    pallas_call x1, Pallas kernels: 4.21 us -> 3.24 us  [finish_panels(): pl.pallas_call(kernel, out_shape=(jax.ShapeDtypeStruct((k_count, OO), F32...]
where the time goes in v4:
time: 92.6 us; the launch traced here: 91.7 us
  blocking collectives  78.7 us (85%)
  Pallas kernels  10.9 us (12%)
  between operations  1.3 us (1%)
    all_to_all x1, blocking collectives, body(): told = lax.all_to_all(shared, 'ta', 0, 0)  31.3 us
    all_to_all x1, blocking collectives, body(): chosen = lax.all_to_all(picked, 'ka', 0, 0).reshape(-1, LANES)  24.6 us
    all_to_all x1, blocking collectives, body(): lax.all_to_all(asked, ('ka', 'ta'), 0, 0, axis_index_groups=groups)  22.8 us
    pallas_call x1, Pallas kernels, sketch_panels(): pl.pallas_call(kernel, out_shape=(jax.ShapeDtypeStruct((rows, LANES), F32...  4.05 us
    pallas_call x1, Pallas kernels, pick_rows(): pl.pallas_call(kernel, out_shape=(jax.ShapeDtypeStruct((ka_count, rows, L...  3.57 us
    pallas_call x1, Pallas kernels, finish_panels(): pl.pallas_call(kernel, out_shape=(jax.ShapeDtypeStruct((k_count, OO), F32...  3.24 us

profile of v4, /device:TPU:6, one launch (start us, length us, event | category | flops | bytes accessed | tf_op | source)
XLA Modules:
  0.0 91.7 jit_solution(9840732344929513000)
XLA Ops:
  1.3 0.7 fusion
  2.0 22.8 %all_to_all.15 = s32[64,1,128]{2,1,0:T(1,128)S(1)} all-to-all(s32[64,1,128]{2,1,0:T(1,128)S(1)} %broadcast_in_dim.16), channel_id=1, replica_groups={{0,8,17,25,32,40,49,57,64,72,81,89,96,104,113,121,130,138,147,155,162,1..., dimensions={0} | all-to-all | bytes 65536 | tf_op jit(solution)/shard_map/all_to_all | solution.py:438
  24.8 3.6 %pick_rows.1 = (bf16[64,32,128]{2,1,0:T(8,128)(2,1)S(1)}, s32[2]{0:T(128)S(1)}, bf16[2,512,256]{2,1,0:T(8,128)(2,1)S(1)}, bf16[64,512]{1,0:T(8,128)(2,1)S(1)}, b...) custom-call(s32[64,128]{1,0:T(8,128)S(1)} %bitcast.7, s32[1]{0:T(128)} %bitcast.2.me, ...), custom_call_target="tpu_custom_call" | custom-call | tf_op jit(solution)/shard_map/pick_rows/pallas_call | solution.py:77
  28.4 24.6 %all_to_all.16 = bf16[64,32,128]{2,1,0:T(8,128)(2,1)S(1)} all-to-all(bf16[64,32,128]{2,1,0:T(8,128)(2,1)S(1)} %get-tuple-element.15), channel_id=1, replica_groups=mesh['ka'=64,'ta'=8] {'ka'}, dimensions={0} | all-to-all | bytes 1048576 | tf_op jit(solution)/shard_map/all_to_all | solution.py:449
  53.1 0.0 copy-start
  53.1 0.0 copy-start.1
  53.1 4.1 %sketch_panels.1 = (f32[256,128]{1,0:T(8,128)S(1)}, bf16[8,384,128]{2,1,0:T(8,128)(2,1)S(1)}) custom-call(s32[2]{0:T(128)S(1)} %get-tuple-element.14.facts, bf16[2048,128]{1,0:T(8,128)(2,1)S(1)} %bitcast.6, bf16[2,256,2048]{2,1,0:T(8,128)(2,1)S(1)} %get-tuple-element.16.near, bf16[2,512,256]{2,1,0:T(8,128)(2,1)S(1)} %get-tuple-element.17.sigma, ...), custom_call_target="tpu_custom_call" | custom-call | tf_op jit(solution)/shard_map/sketch_panels/pallas_call | solution.py:303
  57.1 31.3 %all_to_all.17.told = bf16[8,384,128]{2,1,0:T(8,128)(2,1)S(1)} all-to-all(bf16[8,384,128]{2,1,0:T(8,128)(2,1)S(1)} %get-tuple-element.20), channel_id=1, replica_groups=mesh['ka'=64,'ta'=8] {'ta'}, dimensions={0} | all-to-all | bytes 1572864 | tf_op jit(solution)/shard_map/all_to_all | solution.py:451
  88.4 0.0 copy-done
  88.4 0.0 copy-done.1
  88.4 3.2 %finish_panels.1 = (f32[2,256]{1,0:T(2,128)}, f32[2,64,256]{2,1,0:T(8,128)}, f32[2,64,256]{2,1,0:T(8,128)}) custom-call(bf16[8,384,128]{2,1,0:T(8,128)(2,1)S(1)} %all_to_all.17.told, f32[256,128]{1,0:T(8,128)S(1)} %get-tuple-element.21.sketched, f32[2,256]{1,0:T(2,128)S(1)} %copy-done, f32[2,256]{1,0:T(2,128)S(1)} %copy-done.1), custom_call_target="tpu_custom_call" | custom-call | tf_op jit(solution)/shard_map/finish_panels/pallas_call | solution.py:402
  (1 shorter events, 0.0 us)
Async XLA Ops:
  53.1 35.3 %copy-start = (f32[2,256]{1,0:T(2,128)S(1)}, f32[2,256]{1,0:T(2,128)}, u32[]{:S(2)}) copy-start(f32[2,256]{1,0:T(2,128)} %green.1) | copy-start | bytes 6148
  53.1 35.3 %copy-start.1 = (f32[2,256]{1,0:T(2,128)S(1)}, f32[2,256]{1,0:T(2,128)}, u32[]{:S(2)}) copy-start(f32[2,256]{1,0:T(2,128)} %hamilton.1) | copy-start | bytes 6148

commit v5 on v4

--- a/solution.py
+++ b/solution.py
@@ -22,7 +22,7 @@
 
 
 def turn(place):
-    return ((place >> 1) & 1) | ((place >> 3) & 2)
+    return place if place < 4 else 0
 
 
 def dot(left, right, contract, precision=None):
@@ -49,7 +49,7 @@
         before = jnp.int32(0)
         after = jnp.int32(0)
         length = jnp.int32(0)
-        for place in (0, 2, 16, 18):
+        for place in range(4):
             where_from, amount = told[place, 3], told[place, 2]
             before = before + jnp.where(where_from < me[0], amount, 0)
             after = after + jnp.where(where_from >= me[0], amount, 0)

time: 92.6 us -> 89.5 us (0.967)
  blocking collectives: 78.7 us -> 75.7 us
    all_to_all x1, blocking collectives: 22.8 us -> 18.2 us  [body(): lax.all_to_all(asked, ('ka', 'ta'), 0, 0, axis_index_groups=groups)]
    all_to_all x1, blocking collectives: 24.6 us -> 26.2 us  [body(): chosen = lax.all_to_all(picked, 'ka', 0, 0).reshape(-1, LANES)]
where the time goes in v5:
time: 89.5 us; the launch traced here: 88.6 us
  blocking collectives  75.7 us (85%)
  Pallas kernels  10.9 us (12%)
  between operations  1.3 us (1%)
    all_to_all x1, blocking collectives, body(): told = lax.all_to_all(shared, 'ta', 0, 0)  31.3 us
    all_to_all x1, blocking collectives, body(): chosen = lax.all_to_all(picked, 'ka', 0, 0).reshape(-1, LANES)  26.2 us
    all_to_all x1, blocking collectives, body(): lax.all_to_all(asked, ('ka', 'ta'), 0, 0, axis_index_groups=groups)  18.2 us
    pallas_call x1, Pallas kernels, sketch_panels(): pl.pallas_call(kernel, out_shape=(jax.ShapeDtypeStruct((rows, LANES), F32...  4.05 us
    pallas_call x1, Pallas kernels, pick_rows(): pl.pallas_call(kernel, out_shape=(jax.ShapeDtypeStruct((ka_count, rows, L...  3.57 us
    pallas_call x1, Pallas kernels, finish_panels(): pl.pallas_call(kernel, out_shape=(jax.ShapeDtypeStruct((k_count, OO), F32...  3.25 us

profile of v5, /device:TPU:6, one launch (start us, length us, event | category | flops | bytes accessed | tf_op | source)
XLA Modules:
  0.0 88.6 jit_solution(5903434206134908614)
XLA Ops:
  1.3 0.7 fusion
  2.0 18.2 %all_to_all.15 = s32[64,1,128]{2,1,0:T(1,128)S(1)} all-to-all(s32[64,1,128]{2,1,0:T(1,128)S(1)} %broadcast_in_dim.16), channel_id=1, replica_groups={{0,9,18,27,32,40,48,56,64,72,80,88,96,104,112,120,128,136,144,152,160,1..., dimensions={0} | all-to-all | bytes 65536 | tf_op jit(solution)/shard_map/all_to_all | solution.py:438
  20.2 3.6 %pick_rows.1 = (bf16[64,32,128]{2,1,0:T(8,128)(2,1)S(1)}, s32[2]{0:T(128)S(1)}, bf16[2,512,256]{2,1,0:T(8,128)(2,1)S(1)}, bf16[64,512]{1,0:T(8,128)(2,1)S(1)}, b...) custom-call(s32[64,128]{1,0:T(8,128)S(1)} %bitcast.7, s32[1]{0:T(128)} %bitcast.2.me, ...), custom_call_target="tpu_custom_call" | custom-call | tf_op jit(solution)/shard_map/pick_rows/pallas_call | solution.py:77
  23.8 26.2 %all_to_all.16 = bf16[64,32,128]{2,1,0:T(8,128)(2,1)S(1)} all-to-all(bf16[64,32,128]{2,1,0:T(8,128)(2,1)S(1)} %get-tuple-element.15), channel_id=1, replica_groups=mesh['ka'=64,'ta'=8] {'ka'}, dimensions={0} | all-to-all | bytes 1048576 | tf_op jit(solution)/shard_map/all_to_all | solution.py:449
  50.0 0.0 copy-start
  50.0 0.0 copy-start.1
  50.0 4.0 %sketch_panels.1 = (f32[256,128]{1,0:T(8,128)S(1)}, bf16[8,384,128]{2,1,0:T(8,128)(2,1)S(1)}) custom-call(s32[2]{0:T(128)S(1)} %get-tuple-element.14.facts, bf16[2048,128]{1,0:T(8,128)(2,1)S(1)} %bitcast.6, bf16[2,256,2048]{2,1,0:T(8,128)(2,1)S(1)} %get-tuple-element.16.near, bf16[2,512,256]{2,1,0:T(8,128)(2,1)S(1)} %get-tuple-element.17.sigma, ...), custom_call_target="tpu_custom_call" | custom-call | tf_op jit(solution)/shard_map/sketch_panels/pallas_call | solution.py:303
  54.1 31.3 %all_to_all.17.told = bf16[8,384,128]{2,1,0:T(8,128)(2,1)S(1)} all-to-all(bf16[8,384,128]{2,1,0:T(8,128)(2,1)S(1)} %get-tuple-element.20), channel_id=1, replica_groups=mesh['ka'=64,'ta'=8] {'ta'}, dimensions={0} | all-to-all | bytes 1572864 | tf_op jit(solution)/shard_map/all_to_all | solution.py:451
  85.4 0.0 copy-done
  85.4 0.0 copy-done.1
  85.4 3.2 %finish_panels.1 = (f32[2,256]{1,0:T(2,128)}, f32[2,64,256]{2,1,0:T(8,128)}, f32[2,64,256]{2,1,0:T(8,128)}) custom-call(bf16[8,384,128]{2,1,0:T(8,128)(2,1)S(1)} %all_to_all.17.told, f32[256,128]{1,0:T(8,128)S(1)} %get-tuple-element.21.sketched, f32[2,256]{1,0:T(2,128)S(1)} %copy-done, f32[2,256]{1,0:T(2,128)S(1)} %copy-done.1), custom_call_target="tpu_custom_call" | custom-call | tf_op jit(solution)/shard_map/finish_panels/pallas_call | solution.py:402
  (1 shorter events, 0.0 us)
Async XLA Ops:
  50.0 35.3 %copy-start = (f32[2,256]{1,0:T(2,128)S(1)}, f32[2,256]{1,0:T(2,128)}, u32[]{:S(2)}) copy-start(f32[2,256]{1,0:T(2,128)} %green.1) | copy-start | bytes 6148
  50.0 35.3 %copy-start.1 = (f32[2,256]{1,0:T(2,128)S(1)}, f32[2,256]{1,0:T(2,128)}, u32[]{:S(2)}) copy-start(f32[2,256]{1,0:T(2,128)} %hamilton.1) | copy-start | bytes 6148

commit v6 on v5

--- a/solution.py
+++ b/solution.py
@@ -226,7 +226,14 @@
 
 
 def sketch_panels(facts, chosen, panel, sigma, basis, coef, copies):
-    def kernel(facts, chosen, near, sigma, basis, coef, sketched, shared, panel):
+    def kernel(facts, chosen, near, *refs):
+        far, (sketched, shared, panel), (sigma, basis, coef, sem) = refs[:3], refs[3:6], refs[6:]
+        loads = [
+            pltpu.make_async_copy(far[i], ref, sem.at[i])
+            for i, ref in enumerate((sigma, basis, coef))
+        ]
+        for load in loads:
+            load.start()
         k_count, rows, cols = panel.shape
 
         def history():
@@ -265,6 +272,8 @@
         both = jnp.where(iota((rows, LANES), 1) < R, parts[0], parts[1])
         sketched[...] = both
 
+        for load in loads:
+            load.wait()
         gram = grams(both)
         lane, row = iota((R, LANES), 1), iota((R, LANES), 0)
         left = lane < R
@@ -306,12 +315,18 @@
             jax.ShapeDtypeStruct((rows, LANES), F32),
             jax.ShapeDtypeStruct((copies, told_rows, LANES), BF16),
         ),
-        in_specs=[smem] + [vmem] * 5,
+        in_specs=[smem, vmem, vmem] + [pl.BlockSpec(memory_space=pltpu.HBM)] * 3,
         out_specs=(vmem, vmem),
-        scratch_shapes=[pltpu.VMEM(panel.shape, BF16)],
+        scratch_shapes=[pltpu.VMEM(x.shape, BF16) for x in (panel, sigma, basis, coef)]
+        + [pltpu.SemaphoreType.DMA((3,))],
         compiler_params=pltpu.CompilerParams(vmem_limit_bytes=20 << 20),
         name="sketch_panels",
-    )(facts, chosen, panel, sigma, basis, coef)
+    )(
+        facts,
+        chosen,
+        panel,
+        *[pltpu.with_memory_space_constraint(x, pltpu.HBM) for x in (sigma, basis, coef)],
+    )
 
 
 def finish_panels(told, sketched, green, hamilton, chunk):
@@ -442,12 +457,14 @@
         0,
         axis_index_groups=groups,
     ).reshape(ka_count, LANES)
-    bring = (sigma_history, time_basis.T, history_coef, panel_block)
-    picked, facts, sigma, basis, coef, panel = pick_rows(
+    bring = (panel_block,)
+    picked, facts, panel = pick_rows(
         ka_count, ta_count, told, me, sketch, bring
     )
     chosen = lax.all_to_all(picked, "ka", 0, 0).reshape(-1, LANES)
-    sketched, shared = sketch_panels(facts, chosen, panel, sigma, basis, coef, ta_count)
+    sketched, shared = sketch_panels(
+        facts, chosen, panel, sigma_history, time_basis.T, history_coef, ta_count
+    )
     told = lax.all_to_all(shared, "ta", 0, 0)
     chunk = panel_block.shape[2] // ta_count
     green_next, ortho, right = finish_panels(told, sketched, green_now, hamilton, chunk)

time: 89.5 us -> 90.3 us (level)
    pallas_call x1, Pallas kernels: 4.05 us -> 5.03 us  [sketch_panels(): pl.pallas_call(kernel, out_shape=(jax.ShapeDtypeStruct((rows, LANES), F32...]
where the time goes in v6:
time: 90.3 us; the launch traced here: 89.4 us
  blocking collectives  75.7 us (84%)
  Pallas kernels  11.6 us (13%)
  between operations  1.3 us (1%)
    all_to_all x1, blocking collectives, body(): told = lax.all_to_all(shared, 'ta', 0, 0)  31.3 us
    all_to_all x1, blocking collectives, body(): chosen = lax.all_to_all(picked, 'ka', 0, 0).reshape(-1, LANES)  26.2 us
    all_to_all x1, blocking collectives, body(): lax.all_to_all(asked, ('ka', 'ta'), 0, 0, axis_index_groups=groups)  18.2 us
    pallas_call x1, Pallas kernels, sketch_panels(): pl.pallas_call(kernel, out_shape=(jax.ShapeDtypeStruct((rows, LANES), F32...  5.03 us
    pallas_call x1, Pallas kernels, pick_rows(): pl.pallas_call(kernel, out_shape=(jax.ShapeDtypeStruct((ka_count, rows, L...  3.35 us
    pallas_call x1, Pallas kernels, finish_panels(): pl.pallas_call(kernel, out_shape=(jax.ShapeDtypeStruct((k_count, OO), F32...  3.25 us

profile of v6, /device:TPU:6, one launch (start us, length us, event | category | flops | bytes accessed | tf_op | source)
XLA Modules:
  0.0 89.4 jit_solution(710848825649168545)
XLA Ops:
  1.3 0.7 fusion
  2.0 18.2 %all_to_all.15 = s32[64,1,128]{2,1,0:T(1,128)S(1)} all-to-all(s32[64,1,128]{2,1,0:T(1,128)S(1)} %broadcast_in_dim.16), channel_id=1, replica_groups={{0,9,18,27,32,40,48,56,64,72,80,88,96,104,112,120,128,136,144,152,160,1..., dimensions={0} | all-to-all | bytes 65536 | tf_op jit(solution)/shard_map/all_to_all | solution.py:453
  20.2 3.3 %pick_rows.1 = (bf16[64,32,128]{2,1,0:T(8,128)(2,1)S(1)}, s32[2]{0:T(128)S(1)}, bf16[2,256,2048]{2,1,0:T(8,128)(2,1)S(1)}) custom-call(s32[64,128]{1,0:T(8,128)S(1)} %bitcast.7, s32[1]{0:T(128)} %bitcast.2.me, bf16[16,32,64]{2,1,0:T(8,128)(2,1)} %sketch_far.1, bf16[2,256,2048]{2,1,0:T(8,128)(2,1)} %refs_0_.2), custom_call_target="tpu_custom_call" | custom-call | tf_op jit(solution)/shard_map/pick_rows/pallas_call | solution.py:77
  23.6 26.2 %all_to_all.16 = bf16[64,32,128]{2,1,0:T(8,128)(2,1)S(1)} all-to-all(bf16[64,32,128]{2,1,0:T(8,128)(2,1)S(1)} %get-tuple-element.12), channel_id=1, replica_groups=mesh['ka'=64,'ta'=8] {'ka'}, dimensions={0} | all-to-all | bytes 1048576 | tf_op jit(solution)/shard_map/all_to_all | solution.py:464
  49.8 0.0 copy-start
  49.8 0.0 copy-start.1
  49.8 5.0 %sketch_panels.1 = (f32[256,128]{1,0:T(8,128)S(1)}, bf16[8,384,128]{2,1,0:T(8,128)(2,1)S(1)}) custom-call(s32[2]{0:T(128)S(1)} %get-tuple-element.11.facts, bf16[2048,128]{1,0:T(8,128)(2,1)S(1)} %bitcast.6, bf16[2,256,2048]{2,1,0:T(8,128)(2,1)S(1)} %get-tuple-element.13.near, bf16[2,512,256]{2,1,0:T(8,128)(2,1)} %refs_0_.3, bf16[64,512]{1,0:T(8,128)(2,1)} %bitcast.8, ...), custom_call_target="tpu_custom_call" | custom-call | tf_op jit(solution)/shard_map/sketch_panels/pallas_call | solution.py:312
  54.8 31.3 %all_to_all.17.told = bf16[8,384,128]{2,1,0:T(8,128)(2,1)S(1)} all-to-all(bf16[8,384,128]{2,1,0:T(8,128)(2,1)S(1)} %get-tuple-element.14), channel_id=1, replica_groups=mesh['ka'=64,'ta'=8] {'ta'}, dimensions={0} | all-to-all | bytes 1572864 | tf_op jit(solution)/shard_map/all_to_all | solution.py:468
  86.1 0.0 copy-done
  86.1 0.0 copy-done.1
  86.1 3.3 %finish_panels.1 = (f32[2,256]{1,0:T(2,128)}, f32[2,64,256]{2,1,0:T(8,128)}, f32[2,64,256]{2,1,0:T(8,128)}) custom-call(bf16[8,384,128]{2,1,0:T(8,128)(2,1)S(1)} %all_to_all.17.told, f32[256,128]{1,0:T(8,128)S(1)} %get-tuple-element.15.sketched, f32[2,256]{1,0:T(2,128)S(1)} %copy-done, f32[2,256]{1,0:T(2,128)S(1)} %copy-done.1), custom_call_target="tpu_custom_call" | custom-call | tf_op jit(solution)/shard_map/finish_panels/pallas_call | solution.py:417
  (1 shorter events, 0.0 us)
Async XLA Ops:
  49.8 36.3 %copy-start = (f32[2,256]{1,0:T(2,128)S(1)}, f32[2,256]{1,0:T(2,128)}, u32[]{:S(2)}) copy-start(f32[2,256]{1,0:T(2,128)} %green.1) | copy-start | bytes 6148
  49.8 36.3 %copy-start.1 = (f32[2,256]{1,0:T(2,128)S(1)}, f32[2,256]{1,0:T(2,128)}, u32[]{:S(2)}) copy-start(f32[2,256]{1,0:T(2,128)} %hamilton.1) | copy-start | bytes 6148
